TPU v7x, 128 devices: a whole 4x4x4 slice. The times are simulated.
128 devices in a mesh: section: 2 (over core), grid: 64 (over z, x, y).
Axes of the slice: x: 4, y: 4, z: 4, core: 2. Of those that a mesh axis runs over, the one named last changes fastest.
Arguments:
- visibilities: float32 [2, 6144, 2, 2, 16, 128], P('section', 'grid'), may hold values from -6 to 6
- uv_coords: float32 [6144, 2, 128], P('grid'), may hold values from -8 to 8
- w_terms: float32 [6144], P('grid'), may hold values from -40 to 40
- stations: int32 [2, 6144], P(None, 'grid'), may hold values from 0 to 511
- tile_ids: int32 [6144], P('grid'), may hold values from 0 to 16383, as said below
- owner_map: int32 [16384], replicated, may hold values from 0 to 16383, as said below
- jones_gains: float32 [512, 128], replicated, may hold values from -4.2 to 4.2
Outputs:
- grid_tiles: float32 [2, 16384, 2048], P('section', 'grid')
Inputs may be any that keep to these rules, and one draw needn't show every extreme that they name: `tile_ids`: of the 96 subgrids of one index of grid, at most 4 have tiles held by any one index of grid (index owner_map[tile] // 256), and these lie on at most 2 distinct tiles. `owner_map`: each of 0 to 16383 exactly once.
All inputs are finite; a program needn't handle non-finite values.
Results may differ from a plain program's by a relative error of at most 0.0036.
Values sent between devices are 32-bit elements; how exact they have to be, the bound alone decides.
No kernel may reach another device: no remote copies, remote signals or barrier semaphores. Data moves between devices by JAX's collectives and lax.ppermute only.
A program may use at most 128 MiB of HBM per device.

v0:
```python
import math

import jax
import jax.numpy as jnp
from jax import lax
from jax.sharding import PartitionSpec as P

SUBGRID = 32


def partner_2(x, axis, bit):
    return lax.ppermute(x, axis, [(i, i ^ 1 << bit) for i in range(lax.axis_size(axis))])


def station_gains(station_pair, jones_gains):
    table_rows = jones_gains.shape[0]
    picked = (
        station_pair.reshape(-1)[:, None] == jnp.arange(table_rows, dtype=jnp.int32)[None, :]
    ).astype(jnp.float32)
    looked = jnp.dot(
        picked, jones_gains, precision=lax.Precision.HIGHEST, preferred_element_type=jnp.float32
    )
    return looked.reshape(2, station_pair.shape[1], jones_gains.shape[1] // 8, 2, 2, 2)


def jones_term(vis_rows, gain_p, gain_q):
    total_real = jnp.zeros(vis_rows.shape[:1] + vis_rows.shape[3:], jnp.float32)
    total_imag = jnp.zeros(vis_rows.shape[:1] + vis_rows.shape[3:], jnp.float32)
    for d in range(2):
        coef_real = (gain_p[..., 0] * gain_q[:, :, d, 0] + gain_p[..., 1] * gain_q[:, :, d, 1])[
            ..., None
        ]
        coef_imag = (gain_p[..., 1] * gain_q[:, :, d, 0] - gain_p[..., 0] * gain_q[:, :, d, 1])[
            ..., None
        ]
        vis_real = vis_rows[:, d, 0]
        vis_imag = vis_rows[:, d, 1]
        total_real = total_real + coef_real * vis_real - coef_imag * vis_imag
        total_imag = total_imag + coef_real * vis_imag + coef_imag * vis_real
    return jnp.stack([total_real, total_imag], 1)


def subgrid_tiles(corrected, coords, w_group):
    groups = corrected.shape[0]
    samples = corrected.shape[2]
    steps_t = coords.shape[2]
    chan_count = samples // steps_t
    side = SUBGRID
    freq_scale = 1.0 + jnp.arange(chan_count, dtype=jnp.float32) / (4.0 * chan_count)
    cell_pos = (coords[:, :, None, :] * freq_scale[None, None, :, None]).reshape(groups, 2, samples)
    pixel_pos = jnp.arange(side, dtype=jnp.float32) - side // 2
    phase_angle = 2.0 * jnp.pi / side * cell_pos[:, :, None, :] * pixel_pos[None, None, :, None]
    wave_real = jnp.cos(phase_angle)
    wave_imag = jnp.sin(phase_angle)
    vis_real = corrected[:, 0][:, None, :]
    vis_imag = corrected[:, 1][:, None, :]
    weighted = jnp.concatenate(
        [
            wave_real[:, 0] * vis_real - wave_imag[:, 0] * vis_imag,
            wave_real[:, 0] * vis_imag + wave_imag[:, 0] * vis_real,
        ],
        1,
    ).astype(jnp.bfloat16)
    basis = jnp.concatenate([wave_real[:, 1], wave_imag[:, 1]], 1).astype(jnp.bfloat16)
    product = jnp.einsum("nxk,nyk->nxy", weighted, basis, preferred_element_type=jnp.float32)
    image_real = product[:, :side, :side] - product[:, side:, side:]
    image_imag = product[:, :side, side:] + product[:, side:, :side]
    taper_line = jnp.cos(jnp.pi * pixel_pos / (side + 4.0))
    sine_pos = 0.6 * pixel_pos / side
    n_term = jnp.sqrt(1.0 - sine_pos[:, None] ** 2 - sine_pos[None, :] ** 2) - 1.0
    w_phase = 2.0 * jnp.pi * w_group[:, None, None] * n_term[None]
    norm_scale = taper_line[:, None] * taper_line[None, :] / math.sqrt(samples)
    turn_real = jnp.cos(w_phase) * norm_scale
    turn_imag = jnp.sin(w_phase) * norm_scale
    field_real = image_real * turn_real - image_imag * turn_imag
    field_imag = image_real * turn_imag + image_imag * turn_real
    dft_angle = -2.0 * jnp.pi / side * pixel_pos[:, None] * pixel_pos[None, :]
    dft_real = jnp.cos(dft_angle)
    dft_imag = jnp.sin(dft_angle)
    highest = lax.Precision.HIGHEST

    def apply_right(values, matrix):
        return jnp.einsum("nxy,ly->nxl", values, matrix, precision=highest)

    def apply_left(matrix, values):
        return jnp.einsum("jx,nxl->njl", matrix, values, precision=highest)

    half_real = apply_right(field_real, dft_real) - apply_right(field_imag, dft_imag)
    half_imag = apply_right(field_real, dft_imag) + apply_right(field_imag, dft_real)
    uv_real = apply_left(dft_real, half_real) - apply_left(dft_imag, half_imag)
    uv_imag = apply_left(dft_real, half_imag) + apply_left(dft_imag, half_real)
    return jnp.concatenate([uv_real, uv_imag], 1).reshape(groups, 2 * side * side) / side


def lead_ranks(target, leader, grid_size):
    item_order = jnp.arange(target.shape[0], dtype=jnp.int32)
    lead_hits = (
        (target[:, None] == jnp.arange(grid_size, dtype=jnp.int32)[None, :])
        & (leader == item_order)[:, None]
    ).astype(jnp.int32)
    before = jnp.cumsum(lead_hits, axis=0) - lead_hits
    place_rank = jnp.sum(before * lead_hits, axis=1)
    return place_rank[leader]


def pack_tiles(uv_tiles, target, place_rank, capacity, grid_size):
    row_index = target * capacity + place_rank
    packed_rows = (
        jnp.zeros((grid_size * capacity, uv_tiles.shape[1]), jnp.float32)
        .at[row_index]
        .add(uv_tiles)
    )
    return packed_rows.reshape(grid_size, capacity, uv_tiles.shape[1])


def unpack_tiles(received, every_target, every_slot, every_rank, my_index, tiles_dev):
    grid_size, capacity, width_cols = received.shape
    source = jnp.arange(grid_size, dtype=jnp.int32)[:, None]
    row_index = jnp.where(
        every_target == my_index, source * capacity + every_rank, grid_size * capacity
    )
    slot_table = (
        jnp.full((grid_size * capacity,), tiles_dev, jnp.int32)
        .at[row_index.reshape(-1)]
        .set(every_slot.reshape(-1), mode="drop")
    )
    summed = (
        jnp.zeros((tiles_dev + 1, width_cols), jnp.float32)
        .at[slot_table]
        .add(received.reshape(grid_size * capacity, width_cols))
    )
    return summed[:tiles_dev]


def shards(visibilities, uv_coords, w_terms, stations, tile_ids, owner_map, jones_gains):
    section_index = lax.axis_index("section")
    partner = 1 - section_index
    my_rows = visibilities[0]
    sub_count = my_rows.shape[0]
    chan_count = my_rows.shape[3]
    steps_t = my_rows.shape[4]
    gain_sets = station_gains(stations, jones_gains)
    p_own = lax.dynamic_index_in_dim(gain_sets[0], section_index, 2, keepdims=False)
    q_own = lax.dynamic_index_in_dim(gain_sets[1], section_index, 2, keepdims=False)
    p_self = lax.dynamic_index_in_dim(p_own, section_index, 2, keepdims=False)
    own_term = jones_term(my_rows, p_self, q_own)
    peer_rows = partner_2(visibilities, "section", 0)[0]
    corrected = own_term + jones_term(
        peer_rows, lax.dynamic_index_in_dim(p_own, partner, 2, keepdims=False), q_own
    )
    corrected = corrected.reshape(sub_count, 2, chan_count * steps_t)
    groups = sub_count // 32

    def grid_group(packed):
        return subgrid_tiles(packed[0], packed[1], packed[2])

    uv_tiles = lax.map(
        grid_group,
        (
            corrected.reshape(groups, 32, 2, chan_count * steps_t),
            uv_coords.reshape(groups, 32, 2, steps_t),
            w_terms.reshape(groups, 32),
        ),
    )
    uv_tiles = uv_tiles.reshape(sub_count, -1)
    grid_size = lax.axis_size("grid")
    my_index = lax.axis_index("grid")
    tiles_dev = owner_map.shape[0] // grid_size
    every_tile = lax.all_gather(tile_ids, "grid", axis=0, tiled=True).reshape(grid_size, sub_count)
    every_position = owner_map[every_tile]
    every_target = every_position // tiles_dev
    every_slot = every_position % tiles_dev
    capacity = 3 * sub_count // grid_size
    rank_all = jax.vmap(lambda target, leader: lead_ranks(target, leader, grid_size))
    own_target = lax.dynamic_index_in_dim(every_target, my_index, 0, keepdims=False)
    leaders = jnp.broadcast_to(jnp.arange(sub_count, dtype=jnp.int32), (grid_size, sub_count))
    every_rank = rank_all(every_target, leaders)
    own_rank = lax.dynamic_index_in_dim(every_rank, my_index, 0, keepdims=False)
    received = lax.all_to_all(
        pack_tiles(uv_tiles, own_target, own_rank, capacity, grid_size),
        "grid",
        split_axis=0,
        concat_axis=0,
        tiled=True,
    )
    grid_tiles = unpack_tiles(received, every_target, every_slot, every_rank, my_index, tiles_dev)
    return grid_tiles[None]


def solution(mesh):
    in_specs = (
        P("section", "grid", None, None, None, None),
        P("grid", None, None),
        P("grid"),
        P(None, "grid"),
        P("grid"),
        P(),
        P(),
    )
    out_specs = P("section", "grid", None)
    return jax.shard_map(shards, mesh=mesh, in_specs=in_specs, out_specs=out_specs, check_vma=False)
```

profile of v0, /device:TPU:0, one launch (start us, length us, event | category | flops | bytes accessed | tf_op | source)
XLA Modules:
  0.0 779.5 jit_solution(6530421244104173924)
XLA Ops:
  20.5 350.2 %all-reduce = s32[6144]{0:T(1024)S(1)} all-reduce(s32[6144]{0:T(1024)S(1)} %dynamic-update-slice), channel_id=1, replica_groups=mesh['section'=2,'grid'=64] {'grid'}, use_global_device_ids=true, to_apply=%add | all-reduce | flops 6144 | bytes 49152
  370.9 34.3 %gather_fusion = s32[6144]{0:T(1024)S(1)} fusion(s32[16384]{0:T(1024)S(1)} %copy-done.2, s32[6144]{0:T(1024)S(1)} %broadcast_clamp_fusion), kind=kCustom, calls=%fused_computation | custom fusion | bytes 73728 | tf_op jit(solution)/shard_map/gather | solution.py:170
  405.9 3.3 fusion.55
  409.3 41.1 %gather_fusion.1 = s32[6144]{0:T(1024)S(1)} fusion(s32[64,96]{0,1:T(8,128)S(1)} %fusion.55, s32[6144]{0:T(1024)S(1)} %reshape.729), kind=kCustom, calls=%fused_computation.1 | custom fusion | bytes 98304 | tf_op jit(solution)/shard_map/vmap()/gather | solution.py:103
  451.0 3.6 multiply_subtract_fusion.1
  460.2 2.8 multiply_subtract_fusion
  463.2 275.1 %while.13 = (s32[]{:T(128)}, f32[3,32,2048]{2,1,0:T(8,128)}, f32[3,32,2,128]{3,2,1,0:T(2,128)}, f32[3,32,2,2048]{3,1,2,0:T(8,128)S(1)}, f32[3,32]{1,0:T(4,128)S(1)}, /*index=5*/s32[]{:T(128)}) while((s32[]{:T(128)}, f32[3,32,2048]{2,1,0:T(8,128)}, f32[3,32,2,128]{3,2,1,0:T(2,128)}, f32[3,32,2,2048]{3,1,2,0:T(8,128)S(1)}, ...), condition=%wide.region_4.5_spmd, body=%wide.region_3.4_spmd.sunk | while | flops 692957504 | bytes 104272080 | solution.py:157
  464.5 60.4 %multiply_sine_fusion.4 = (f32[32,2,32,2048]{3,2,0,1:T(8,128)S(1)}, f32[32,2,32,2048]{3,2,0,1:T(8,128)}) fusion(f32[32]{0:T(128)S(1)} %iota_add_fusion.2, f32[32,2,2048]{2,0,1:T(8,128)S(1)} %multiply_multiply_fusion.8), kind=kLoop, calls=%fused_computation.5.clone.1 | loop fusion | flops 4194304 | bytes 34078848 | tf_op jit(solution)/shard_map/while/body/eval_jaxpr/sin | solution.py:54
  524.9 6.7 subtract_convert_fusion.2
  531.6 6.2 fusion.130
  537.8 5.9 fusion.131
  556.1 60.4 %multiply_sine_fusion.4 = (f32[32,2,32,2048]{3,2,0,1:T(8,128)S(1)}, f32[32,2,32,2048]{3,2,0,1:T(8,128)}) fusion(f32[32]{0:T(128)S(1)} %iota_add_fusion.2, f32[32,2,2048]{2,0,1:T(8,128)S(1)} %multiply_multiply_fusion.8), kind=kLoop, calls=%fused_computation.5.clone.1 | loop fusion | flops 4194304 | bytes 34078848 | tf_op jit(solution)/shard_map/while/body/eval_jaxpr/sin | solution.py:54
  616.6 6.7 subtract_convert_fusion.2
  623.2 6.2 fusion.130
  629.4 5.9 fusion.131
  635.6 2.4 fusion.132
  647.7 60.4 %multiply_sine_fusion.4 = (f32[32,2,32,2048]{3,2,0,1:T(8,128)S(1)}, f32[32,2,32,2048]{3,2,0,1:T(8,128)}) fusion(f32[32]{0:T(128)S(1)} %iota_add_fusion.2, f32[32,2,2048]{2,0,1:T(8,128)S(1)} %multiply_multiply_fusion.8), kind=kLoop, calls=%fused_computation.5.clone.1 | loop fusion | flops 4194304 | bytes 34078848 | tf_op jit(solution)/shard_map/while/body/eval_jaxpr/sin | solution.py:54
  708.2 6.7 subtract_convert_fusion.2
  714.9 6.2 fusion.130
  721.1 5.9 fusion.131
  738.3 2.9 scatter_custom_fusion.1
  742.8 4.8 all-to-all-start
  748.0 23.0 %scatter_custom_fusion = s32[256]{0:T(256)S(1)} fusion(s32[6144]{0:T(1024)S(1)} %bitcast.216, s32[6144]{0:T(1024)S(1)} %add_select_fusion.1, s32[]{:T(128)} %constant.218.clone.1), kind=kCustom, calls=%fused_computation.152 | custom fusion | bytes 1028 | tf_op jit(solution)/shard_map/scatter | solution.py:125
  772.8 5.3 scatter_custom_fusion.2
  (196 shorter events, 66.7 us)
Async XLA Ops:
  0.0 1.0 copy-start
  0.0 454.7 %collective-permute-start = (f32[1,96,2,2,16,128]{5,4,3,2,1,0:T(8,128)}, f32[1,96,2,2,16,128]{5,4,3,2,1,0:T(8,128)}, u32[]{:S(2)}, u32[]{:S(2)}) collective-permute-start(f32[1,96,2,2,16,128]{5,4,3,2,1,0:T(8,128)} %param.9), channel_id=1, source_target_pairs={{0,64},{64,0},{1,65},{65,1},{2,66},{66,2},{3,67},{67,3},{4,68},{68... | collective-permute-start | bytes 9437192 | tf_op jit(solution)/shard_map/ppermute | solution.py:12
  14.8 4.1 copy-start.15
  14.8 4.2 copy-start.17
  14.9 5.4 copy-start.16
  14.9 356.0 %copy-start.2 = (s32[16384]{0:T(1024)S(1)}, s32[16384]{0:T(1024)}, u32[]{:S(2)}) copy-start(s32[16384]{0:T(1024)} %param.14) | copy-start | bytes 196612
  405.2 0.6 copy-start.11
  409.2 41.8 %copy-start.7 = (f32[3,32,1,2048]{3,1,2,0:T(8,128)S(1)}, f32[3,32,1,2048]{3,1,2,0:T(8,128)}, u32[]{:S(2)}) copy-start(f32[3,32,1,2048]{3,1,2,0:T(8,128)} %mul.736) | copy-start | bytes 2359300
  409.2 41.8 %copy-start.8 = (f32[3,32,1,2048]{3,1,2,0:T(8,128)S(1)}, f32[3,32,1,2048]{3,1,2,0:T(8,128)}, u32[]{:S(2)}) copy-start(f32[3,32,1,2048]{3,1,2,0:T(8,128)} %mul.742) | copy-start | bytes 2359300
  409.2 41.8 %copy-start.9 = (f32[3,32,1,2048]{3,1,2,0:T(8,128)S(1)}, f32[3,32,1,2048]{3,1,2,0:T(8,128)}, u32[]{:S(2)}) copy-start(f32[3,32,1,2048]{3,1,2,0:T(8,128)} %mul.748) | copy-start | bytes 2359300
  409.3 41.8 %copy-start.10 = (f32[3,32,1,2048]{3,1,2,0:T(8,128)S(1)}, f32[3,32,1,2048]{3,1,2,0:T(8,128)}, u32[]{:S(2)}) copy-start(f32[3,32,1,2048]{3,1,2,0:T(8,128)} %mul.754) | copy-start | bytes 2359300
  450.5 4.2 copy-start.13
  457.8 2.1 copy-start.5
  458.8 1.4 copy-start.6
  460.2 2.8 copy-start.3
  460.2 2.9 copy-start.4
  742.8 4.9 copy-start.14
  742.8 5.0 copy-start.12
  742.8 28.2 %all-to-all-start = ((f32[64,4,2048]{2,1,0:T(4,128)}), f32[64,4,2048]{2,1,0:T(4,128)S(1)}, u32[]{:S(2)}, u32[]{:S(2)}) async-start(f32[64,4,2048]{2,1,0:T(4,128)} %reshape.719), calls=%async_computation | async-start | bytes 4194304 | tf_op jit(solution)/shard_map/all_to_all | solution.py:179
  771.0 8.5 %copy-start.1 = (f32[512,128]{1,0:T(8,128)S(1)}, f32[512,128]{1,0:T(8,128)}, u32[]{:S(2)}) copy-start(f32[512,128]{1,0:T(8,128)} %param.15) | copy-start | bytes 786436
where the time goes:
time: 780 us
  blocking collectives  350 us (45%)
  other arithmetic  229 us (29%)
  local copies, waits for them, and re-layouts  155 us (20%)
  matrix products  38.7 us (5%)
    unnamed x1, blocking collectives  350 us
    sin x3, other arithmetic, subgrid_tiles(): wave_imag = jnp.sin(phase_angle)  181 us
    gather x3, local copies, waits for them, and re-layouts, lead_ranks(): return place_rank[leader]  41.3 us
    gather x2, local copies, waits for them, and re-layouts, shards(): every_position = owner_map[every_tile]  34.4 us
    scatter x1, local copies, waits for them, and re-layouts, unpack_tiles(): slot_table = jnp.full((grid_size * capacity,), tiles_dev, jnp.int32).at[r...  23 us
    another operation x3, other arithmetic  20 us
    squeeze x3, local copies, waits for them, and re-layouts, subgrid_tiles(): wave_real[:, 1]  18.6 us
    dot_general x3, matrix products, subgrid_tiles(): jnp.einsum('nxk,nyk->nxy', weighted, basis, preferred_element_type=jnp.fl...  17.8 us
  transfers between devices with their start and end apart: 2, of which 0 were waited for; matrix products, arithmetic and copies ran while one was open for 16% of the time, Pallas kernels for 0%

commit v1 on v0

v1 whole, which is shorter than its diff:
```python
import math

import numpy as np
import jax
import jax.numpy as jnp
from jax import lax
from jax.experimental import pallas as pl
from jax.experimental.pallas import tpu as pltpu
from jax.sharding import PartitionSpec as P

SIDE = 32
HALF = 16
CHUNKS = 2
GROUP = 4

PIXELS = np.concatenate([np.arange(16), -1 - np.arange(16)]).astype(np.float64)


def fit_even(function, reach, terms):
    nodes = np.cos(np.pi * (np.arange(64) + 0.5) / 64)
    square = (nodes + 1.0) / 2.0 * reach * reach
    cheb = np.polynomial.chebyshev.chebfit(nodes, function(np.sqrt(square)), terms - 1)
    poly = np.polynomial.chebyshev.cheb2poly(cheb)
    shift = np.polynomial.polynomial.Polynomial(poly)(
        np.polynomial.polynomial.Polynomial([-1.0, 2.0 / (reach * reach)])
    )
    return [float(np.float32(value)) for value in shift.coef]


def sinc_turns(scale):
    return lambda x: np.where(x > 0, np.sin(scale * x) / np.maximum(x, 1e-30), scale)


HALF_SIN = fit_even(sinc_turns(np.pi), 0.5, 6)
HALF_COS = fit_even(lambda x: np.cos(np.pi * x), 0.5, 6)
STEP_SIN = fit_even(sinc_turns(2 * np.pi), 0.0625, 4)
STEP_COS = fit_even(lambda x: np.cos(2 * np.pi * x), 0.0625, 4)


def horner(coefs, square):
    total = square * coefs[-1] + coefs[-2]
    for value in coefs[-3::-1]:
        total = total * square + value
    return total


def sincos_half(x):
    square = x * x
    half_sin = x * horner(HALF_SIN, square)
    half_cos = horner(HALF_COS, square)
    twice = half_sin + half_sin
    return twice * half_cos, 1.0 - twice * half_sin


def sincos_step(x):
    square = x * x
    return x * horner(STEP_SIN, square), horner(STEP_COS, square)


def spread(ref, g, k, c):
    line = ref[g, k, pl.ds(c, 8, stride=0), :]
    return jnp.concatenate([line, line], 0)


def split_hi_lo(values):
    high = values.astype(jnp.bfloat16)
    low = (values - high.astype(jnp.float32)).astype(jnp.bfloat16)
    return high, low


def np_split(values):
    high = np.asarray(values, np.float32).astype(jnp.bfloat16)
    low = (np.asarray(values, np.float32) - high.astype(np.float32)).astype(jnp.bfloat16)
    return high, low


def tables(samples):
    lane = np.arange(128)
    lane_ri, lane_pol, lane_pix = lane // 64, (lane // 32) % 2, lane % 32
    row_p = PIXELS[:, None]
    lane_p = PIXELS[lane_pix][None, :]
    sine_row, sine_lane = 0.6 * row_p / SIDE, 0.6 * lane_p / SIDE
    n_term = np.sqrt(1.0 - sine_row**2 - sine_lane**2) - 1.0
    taper = np.cos(np.pi * row_p / (SIDE + 4.0)) * np.cos(np.pi * lane_p / (SIDE + 4.0))
    norm = taper / math.sqrt(samples) / SIDE
    signed = norm * np.where(lane_ri == 0, -1.0, 1.0)[None, :]
    pixel_tables = np.stack([n_term, norm, signed]).astype(np.float32)

    freq = np.arange(SIDE) - SIDE // 2
    angle = 2.0 * np.pi / SIDE * PIXELS[:, None] * freq[None, :]
    cos_t, sin_t = np.cos(angle), np.sin(angle)
    right = np.zeros((2, 2, 32, 2, 2, 2, 32))
    for pol in range(2):
        re_re, re_im = cos_t, -sin_t
        im_re, im_im = sin_t, cos_t
        right[0, pol, :, 0, 0, pol, :] = re_re
        right[0, pol, :, 0, 1, pol, :] = re_im
        right[1, pol, :, 0, 0, pol, :] = im_re
        right[1, pol, :, 0, 1, pol, :] = im_im
        right[0, pol, :, 1, 0, pol, :] = re_im
        right[0, pol, :, 1, 1, pol, :] = -re_re
        right[1, pol, :, 1, 0, pol, :] = im_im
        right[1, pol, :, 1, 1, pol, :] = -im_re
    right_high, right_low = np_split(right.reshape(128, 256))
    right_all = np.concatenate([right_high, right_high, right_low], 0)

    order = np.arange(SIDE).reshape(8, 4).T.reshape(-1)
    angle = 2.0 * np.pi / SIDE * freq[order][:, None] * PIXELS[None, :]
    left = np.concatenate([np.cos(angle), np.sin(angle)], 1)
    left_high, left_low = np_split(left)
    left_all = np.concatenate([left_high, left_high, left_low], 1)
    return pixel_tables, right_all, left_all


def prep_kernel(section_ref, stations_ref, tile_ref, owner_ref, jones_ref, coef_ref, row_ref, slot_ref,
                p_rows, q_rows, turned, first_ref):
    section = section_ref[0]
    sub_count = stations_ref.shape[1]
    half = sub_count // 2
    tiles_dev = owner_ref.shape[0] // (slot_ref.shape[0] // 2)
    p_rows[...] = jnp.zeros_like(p_rows)
    q_rows[...] = jnp.zeros_like(q_rows)

    def fetch(step, carry):
        item = section * half + step
        p_rows[pl.ds(step, 1), :] = jones_ref[pl.ds(stations_ref[0, item], 1), :]
        q_rows[pl.ds(step, 1), :] = jones_ref[pl.ds(stations_ref[1, item], 1), :]
        return carry

    lax.fori_loop(0, half, fetch, 0)
    lane = lax.broadcasted_iota(jnp.int32, (128, 128), 1)
    odd = (lane & 1) == 1
    high_pair = (lane & 2) == 2

    def swap_one(x):
        return jnp.where(odd, pltpu.roll(x, 1, 1), pltpu.roll(x, 127, 1))

    def swap_two(x):
        return jnp.where(high_pair, pltpu.roll(x, 2, 1), pltpu.roll(x, 126, 1))

    gain_p = p_rows[...]
    gain_p_turned = swap_one(gain_p)
    for kind in range(2):
        gain_q = q_rows[...] if kind == 0 else swap_two(q_rows[...])
        straight = gain_p * gain_q
        crossed = gain_p_turned * gain_q
        real = straight + swap_one(straight)
        imag = swap_one(crossed) - crossed
        turned[...] = jnp.where(odd, imag, real).T
        for place in range(8):
            coef_ref[kind * 8 + place] = turned[pl.ds(place, 16, stride=8), :]

    def clear(step, carry):
        slot_ref[2 * step] = -1
        slot_ref[2 * step + 1] = -1
        return carry

    lax.fori_loop(0, slot_ref.shape[0] // 2, clear, 0)

    def place_item(item, carry):
        position = owner_ref[tile_ref[item]]
        target = position // tiles_dev
        slot = position % tiles_dev
        first = slot_ref[2 * target]
        rank = jnp.where((first == -1) | (first == slot), 0, 1)
        slot_ref[2 * target + rank] = slot
        row_ref[item] = 2 * target + rank
        return carry

    lax.fori_loop(0, sub_count, place_item, 0)


def grid_kernel(chunk_size, chunk, section_ref, w_ref, coef_ref, own_ref, peer_ref, uv_ref, pixel_ref, right_ref,
                left_ref, mine_ref, other_ref, bcast):
    section = section_ref[0]
    step = pl.program_id(0)
    base = chunk * chunk_size + step * GROUP
    half = w_ref.shape[0] // 2
    lane = lax.broadcasted_iota(jnp.int32, (16, 128), 1)
    lane8 = lax.broadcasted_iota(jnp.int32, (8, 128), 1)
    upper = (lane & 16) == 16
    sign = jnp.where(upper, -1.0, 1.0)
    re_lane = lane < 64
    sign_p = jnp.where(re_lane, -sign, sign)
    sign_q = jnp.where(re_lane, -1.0, 1.0)
    q_index = (lax.broadcasted_iota(jnp.int32, (16, 128), 0).astype(jnp.float32) + 0.5) / SIDE
    chan = lax.broadcasted_iota(jnp.int32, (16, 128), 0).astype(jnp.float32)
    chan_half = (1.0 + chan / 64.0) / (2.0 * SIDE)
    shift = lax.rem(128 - base, 128)

    coefs = {}
    for kind in range(2):
        for pol in range(2):
            for row in range(2):
                for part in range(2):
                    place = kind * 8 + (pol ^ section) * 4 + (row ^ section) * 2 + part
                    coefs[kind, pol, row, part] = pltpu.roll(coef_ref[place], shift, 1)

    fields = []
    for g in range(GROUP):
        corr = [[None, None], [None, None]]
        for row in range(2):
            for kind in range(2):
                column = (row ^ section) ^ kind
                if row == 0:
                    vis = [own_ref[0, g, column, 0], own_ref[0, g, column, 1]]
                else:
                    vis = [peer_ref[g, column, 0], peer_ref[g, column, 1]]
                for pol in range(2):
                    cr = jnp.broadcast_to(coefs[kind, pol, row, 0][:, g : g + 1], (16, 128))
                    ci = jnp.broadcast_to(coefs[kind, pol, row, 1][:, g : g + 1], (16, 128))
                    real = cr * vis[0] - ci * vis[1]
                    imag = cr * vis[1] + ci * vis[0]
                    if corr[pol][0] is None:
                        corr[pol] = [real, imag]
                    else:
                        corr[pol] = [corr[pol][0] + real, corr[pol][1] + imag]
        u_row = jnp.broadcast_to(uv_ref[g, 0:1, :], (16, 128))
        v_row = jnp.broadcast_to(uv_ref[g, 1:2, :], (16, 128))
        turn_sin, turn_cos = sincos_half((u_row + v_row) * chan_half)
        for pol in range(2):
            real, imag = corr[pol]
            bcast[g, pol] = real * turn_cos + imag * turn_sin
            bcast[g, 2 + pol] = imag * turn_cos - real * turn_sin

        waves = []
        for cell in (u_row, v_row):
            turns = cell * q_index
            sin_0, cos_0 = sincos_half(turns - jnp.round(turns))
            sin_d, cos_d = sincos_step(turns * (1.0 / 64.0))
            cos_1 = cos_0 * cos_d - sin_0 * sin_d
            sin_1 = sin_0 * cos_d + cos_0 * sin_d
            waves.append([cos_0, sin_0, cos_1, sin_1, cos_d + cos_d])
        total = None
        for pair in range(8):
            left_parts, right_parts = [], []
            for c in (2 * pair, 2 * pair + 1):
                cos_u, sin_u = waves[0][0], waves[0][1]
                cos_v, sin_v = waves[1][0], waves[1][1]
                left_parts.append(jnp.concatenate([cos_u.astype(jnp.bfloat16), sin_u.astype(jnp.bfloat16)], 0))
                pieces = []
                for k in range(4):
                    line = spread(bcast, g, k, c)
                    pieces.append((cos_v * line).astype(jnp.bfloat16))
                    pieces.append((sin_v * line).astype(jnp.bfloat16))
                right_parts.append(jnp.concatenate(pieces, 0))
                for wave in waves:
                    cos_0, sin_0, cos_1, sin_1, twice = wave
                    wave[0], wave[1] = cos_1, sin_1
                    if c < 14:
                        wave[2], wave[3] = twice * cos_1 - cos_0, twice * sin_1 - sin_0
            part = lax.dot_general(
                jnp.concatenate(left_parts, 1),
                jnp.concatenate(right_parts, 1),
                (((1,), (1,)), ((), ())),
                preferred_element_type=jnp.float32,
            )
            total = part if total is None else total + part

        x_rows, y_rows = total[:16], total[16:]
        x_cos = jnp.where(upper, pltpu.roll(x_rows, 16, 1), x_rows)
        x_sin = jnp.where(upper, x_rows, pltpu.roll(x_rows, 112, 1))
        y_cos = jnp.where(upper, pltpu.roll(y_rows, 16, 1), y_rows)
        y_sin = jnp.where(upper, y_rows, pltpu.roll(y_rows, 112, 1))
        even = x_cos + sign_p * pltpu.roll(x_sin, 64, 1)
        oddp = sign_q * pltpu.roll(y_cos, 64, 1) - sign * y_sin
        image = jnp.concatenate([even + oddp, even - oddp], 0)

        w_turns = w_ref[section * half + base + g] * pixel_ref[0]
        w_sin, w_cos = sincos_half(w_turns - jnp.round(w_turns))
        fields.append(
            image * (w_cos * pixel_ref[1]) + pltpu.roll(image, 64, 1) * (w_sin * pixel_ref[2])
        )

    high, low = split_hi_lo(jnp.concatenate(fields, 0))
    rows = jnp.dot(
        jnp.concatenate([high, low, high], 1), right_ref[...], preferred_element_type=jnp.float32
    )
    for g in range(GROUP):
        high, low = split_hi_lo(rows[g * 32 : (g + 1) * 32])
        stack = jnp.concatenate(
            [high[:, :128], high[:, 128:], low[:, :128], low[:, 128:], high[:, :128], high[:, 128:]], 0
        )
        uv = jnp.dot(left_ref[...], stack, preferred_element_type=jnp.float32)
        part = [uv[k * 8 : (k + 1) * 8] for k in range(4)]
        below = lane8 < 64
        quarter = (lane8 & 32) == 32
        a0 = jnp.where(below, part[0], pltpu.roll(part[2], 64, 1))
        a2 = jnp.where(below, pltpu.roll(part[0], 64, 1), part[2])
        a1 = jnp.where(below, part[1], pltpu.roll(part[3], 64, 1))
        a3 = jnp.where(below, pltpu.roll(part[1], 64, 1), part[3])
        mine_ref[g, 0:8, :] = jnp.where(quarter, pltpu.roll(a1, 32, 1), a0)
        other_ref[g, 0:8, :] = jnp.where(quarter, a1, pltpu.roll(a0, 96, 1))
        mine_ref[g, 8:16, :] = jnp.where(quarter, pltpu.roll(a3, 32, 1), a2)
        other_ref[g, 8:16, :] = jnp.where(quarter, a3, pltpu.roll(a2, 96, 1))


def pack_kernel(section_ref, row_ref, *refs):
    count = (len(refs) - 1) // 2
    packed = refs[-1]
    section = section_ref[0]
    half = row_ref.shape[0] // 2
    packed[...] = jnp.zeros_like(packed)
    for side in range(2):
        start = (section ^ side) * half
        for part in range(count):
            values = refs[side * count + part]
            size = values.shape[0]
            offset = start + part * size

            def add(item, carry, values=values, offset=offset):
                row = row_ref[offset + item]
                packed[row] = packed[row] + values[item]
                return carry

            lax.fori_loop(0, size, add, 0)


def unpack_kernel(slot_ref, received_ref, out_ref, acc):
    tiles_dev = out_ref.shape[0]
    acc[...] = jnp.zeros_like(acc)

    def add(item, carry):
        slot = slot_ref[item]
        start = pl.multiple_of(jnp.where(slot < 0, tiles_dev, slot) * 16, 16)
        acc[pl.ds(start, 16), :] = acc[pl.ds(start, 16), :] + received_ref[item]
        return carry

    lax.fori_loop(0, slot_ref.shape[0], add, 0)

    def turn(block, carry):
        top = pl.multiple_of(block * 8, 8)
        for column in range(16):
            out_ref[pl.ds(top, 8), column * 128 : (column + 1) * 128] = acc[
                pl.ds(top * 16 + column, 8, stride=16), :
            ]
        return carry

    lax.fori_loop(0, tiles_dev // 8, turn, 0)


SMEM = pl.BlockSpec(memory_space=pltpu.SMEM)
VMEM = pl.BlockSpec(memory_space=pltpu.VMEM)


def prep(section, stations, tile_ids, owner_map, jones_gains, grid_size):
    return pl.pallas_call(
        prep_kernel,
        out_shape=(
            jax.ShapeDtypeStruct((16, 16, 128), jnp.float32),
            jax.ShapeDtypeStruct(tile_ids.shape, jnp.int32),
            jax.ShapeDtypeStruct((2 * grid_size,), jnp.int32),
        ),
        in_specs=[SMEM, SMEM, SMEM, SMEM, VMEM],
        out_specs=(VMEM, SMEM, SMEM),
        scratch_shapes=[pltpu.VMEM((128, 128), jnp.float32)] * 3 + [pltpu.SMEM((8,), jnp.int32)],
        cost_estimate=pl.CostEstimate(flops=10_000_000, bytes_accessed=500_000, transcendentals=0),
        name="prep",
    )(section, stations, tile_ids, owner_map, jones_gains)


def grid_chunk(chunk, chunk_size, half, section, w_terms, coefs, visibilities, peer, uv_coords, constants):
    per_half = half // GROUP
    offset = chunk * chunk_size // GROUP

    def fixed(shape):
        return pl.BlockSpec(shape, lambda i, s, w: (0,) * len(shape))

    out = jax.ShapeDtypeStruct((chunk_size, 16, 128), jnp.float32)
    return pl.pallas_call(
        lambda *refs: grid_kernel(chunk_size, chunk, *refs),
        out_shape=(out, out),
        grid_spec=pltpu.PrefetchScalarGridSpec(
            num_scalar_prefetch=2,
            grid=(chunk_size // GROUP,),
            in_specs=[
                fixed((16, 16, 128)),
                pl.BlockSpec(
                    (1, GROUP, 2, 2, 16, 128), lambda i, s, w: (0, s[0] * per_half + offset + i, 0, 0, 0, 0)
                ),
                pl.BlockSpec((GROUP, 2, 2, 16, 128), lambda i, s, w: (i, 0, 0, 0, 0)),
                pl.BlockSpec((GROUP, 2, 128), lambda i, s, w: (s[0] * per_half + offset + i, 0, 0)),
                fixed((3, 32, 128)),
                fixed((384, 256)),
                fixed((32, 192)),
            ],
            out_specs=[pl.BlockSpec((GROUP, 16, 128), lambda i, s, w: (i, 0, 0))] * 2,
            scratch_shapes=[pltpu.VMEM((GROUP, 4, 16, 128), jnp.float32)],
        ),
        cost_estimate=pl.CostEstimate(
            flops=chunk_size * 300_000_000, bytes_accessed=chunk_size * 100_000, transcendentals=0
        ),
        name="grid_chunk",
    )(section, w_terms, coefs, visibilities, peer, uv_coords, *constants)


def shards(visibilities, uv_coords, w_terms, stations, tile_ids, owner_map, jones_gains):
    sub_count = visibilities.shape[1]
    samples = visibilities.shape[4] * visibilities.shape[5]
    half = sub_count // 2
    chunk_size = half // CHUNKS
    grid_size = lax.axis_size("grid")
    tiles_dev = owner_map.shape[0] // grid_size
    section_index = lax.axis_index("section").astype(jnp.int32)
    section = section_index.reshape(1)
    swap = [(0, 1), (1, 0)]

    peers = []
    for chunk in range(CHUNKS):
        start = (1 - section_index) * half + chunk * chunk_size
        rows = lax.dynamic_slice_in_dim(visibilities[0], start, chunk_size, 0)
        peers.append(lax.ppermute(rows, "section", swap))

    coefs, row_index, slots = prep(section, stations, tile_ids, owner_map, jones_gains, grid_size)
    every_slot = lax.all_to_all(
        slots.reshape(grid_size, 2), "grid", split_axis=0, concat_axis=0, tiled=True
    ).reshape(-1)

    constants = [jnp.asarray(table) for table in tables(samples)]
    mine, theirs = [], []
    for chunk in range(CHUNKS):
        kept, other = grid_chunk(
            chunk, chunk_size, half, section, w_terms, coefs, visibilities, peers[chunk], uv_coords, constants
        )
        mine.append(kept)
        theirs.append(lax.ppermute(other, "section", swap))

    packed = pl.pallas_call(
        pack_kernel,
        out_shape=jax.ShapeDtypeStruct((2 * grid_size, 16, 128), jnp.float32),
        in_specs=[SMEM, SMEM] + [VMEM] * (2 * CHUNKS),
        out_specs=VMEM,
        name="pack",
    )(section, row_index, *mine, *theirs)
    received = lax.all_to_all(
        packed.reshape(grid_size, 2, 16, 128), "grid", split_axis=0, concat_axis=0, tiled=True
    ).reshape(2 * grid_size, 16, 128)
    tiles = pl.pallas_call(
        unpack_kernel,
        out_shape=jax.ShapeDtypeStruct((tiles_dev, 2048), jnp.float32),
        in_specs=[SMEM, VMEM],
        out_specs=VMEM,
        scratch_shapes=[pltpu.VMEM(((tiles_dev + 1) * 16, 128), jnp.float32)],
        name="unpack",
    )(every_slot, received)
    return tiles[None]


def solution(mesh):
    in_specs = (
        P("section", "grid", None, None, None, None),
        P("grid", None, None),
        P("grid"),
        P(None, "grid"),
        P("grid"),
        P(),
        P(),
    )
    out_specs = P("section", "grid", None)
    return jax.shard_map(shards, mesh=mesh, in_specs=in_specs, out_specs=out_specs, check_vma=False)
```

time: 780 us -> 85.9 us (0.11)
  blocking collectives: 350 us -> 0 us
  other arithmetic: 229 us -> 0.7 us
  local copies, waits for them, and re-layouts: 155 us -> 6.96 us
  matrix products: 38.7 us -> 0 us
  Pallas kernels: 0 us -> 38.2 us
  waiting for transfers between devices: 0.01 us -> 21.8 us
  starting transfers between devices: 4.83 us -> 17.7 us
    unnamed x1 -> x0, blocking collectives: 350 us -> none
    sin x3 -> x0, other arithmetic: 181 us -> none  [subgrid_tiles(): wave_imag = jnp.sin(phase_angle)]
    gather x5 -> x0, local copies, waits for them, and re-layouts: 75.6 us -> none  [the longest x3 41.3 us: lead_ranks(): return place_rank[leader]]
    dot_general x28 -> x0, matrix products: 38.7 us -> none  [the longest x3 17.8 us: subgrid_tiles(): jnp.einsum('nxk,nyk->nxy', weighted, basis, preferred_element_type=jnp.fl...]
    pallas_call x0 -> x5, Pallas kernels: none -> 38.2 us  [the longest x2 25 us: grid_chunk(): pl.pallas_call(lambda *refs: grid_kernel(chunk_size, chunk, *refs), out_s...]
    squeeze x15 -> x0, local copies, waits for them, and re-layouts: 25.9 us -> none  [the longest x3 18.6 us: subgrid_tiles(): wave_real[:, 1]]
    another operation x4 -> x0, other arithmetic: 23.3 us -> none
    scatter x1 -> x0, local copies, waits for them, and re-layouts: 23 us -> none  [unpack_tiles(): slot_table = jnp.full((grid_size * capacity,), tiles_dev, jnp.int32).at[r...]
  transfers between devices with their start and end apart: 2 -> 6, of which waited for: 0 -> 2; matrix products, arithmetic and copies ran while one was open for 16% -> 2% of each run, Pallas kernels for 0% -> 39%
where the time goes in v1:
time: 85.9 us; the launch traced here: 85.4 us
  Pallas kernels  38.2 us (44%)
  waiting for transfers between devices  21.8 us (25%)
  starting transfers between devices  17.7 us (21%)
  local copies, waits for them, and re-layouts  6.96 us (8%)
    pallas_call x2, Pallas kernels, grid_chunk(): pl.pallas_call(lambda *refs: grid_kernel(chunk_size, chunk, *refs), out_s...  25 us
    all_to_all x1, waiting for transfers between devices, shards(): lax.all_to_all(packed.reshape(grid_size, 2, 16, 128), 'grid', split_axis=...  16 us
    all_to_all x1, starting transfers between devices, shards(): lax.all_to_all(slots.reshape(grid_size, 2), 'grid', split_axis=0, concat_...  11.5 us
    all_to_all x1, waiting for transfers between devices, shards(): lax.all_to_all(slots.reshape(grid_size, 2), 'grid', split_axis=0, concat_...  5.86 us
    pallas_call x1, Pallas kernels, prep(): pl.pallas_call(prep_kernel, out_shape=(jax.ShapeDtypeStruct((16, 16, 128)...  5.71 us
    all_to_all x1, starting transfers between devices, shards(): lax.all_to_all(packed.reshape(grid_size, 2, 16, 128), 'grid', split_axis=...  4.97 us
    pallas_call x1, Pallas kernels, shards(): pl.pallas_call(unpack_kernel, out_shape=jax.ShapeDtypeStruct((tiles_dev,...  4.54 us
    unnamed x12, local copies, waits for them, and re-layouts  3.46 us
  transfers between devices with their start and end apart: 6, of which 2 were waited for; matrix products, arithmetic and copies ran while one was open for 2% of the time, Pallas kernels for 39%

profile of v1, /device:TPU:0, one launch (start us, length us, event | category | flops | bytes accessed | tf_op | source)
XLA Modules:
  0.0 85.4 jit_solution(2037315897947826271)
XLA Ops:
  0.0 1.5 %dynamic-slice_bitcast_fusion = (f32[24,2,2,16,128]{4,3,2,1,0:T(8,128)S(1)}, f32[24,2,2,16,128]{4,3,2,1,0:T(8,128)S(1)}) fusion(f32[1,96,2,2,16,128]{5,4,3,2,1,0:T(8,128)} %refs_3_.3, s32[]{:T(128)S(6)} %select_n.7, s32[]{:T(128)S(6)} %select_n.6), kind=kLoop, calls=%fused_computation | loop fusion | bytes 3145736 | tf_op jit(solution)/shard_map/dynamic_slice | solution.py:411
  1.5 0.1 collective-permute-start.1
  1.6 0.5 collective-permute-start
  2.1 5.7 %prep.1 = (f32[16,16,128]{2,1,0:T(8,128)}, s32[96]{0:T(128)}, s32[128]{0:T(128)}) custom-call(s32[1]{0:T(128)} %bitcast.section_ref.refs_0_, s32[2,96]{1,0:T(2,128)} %stations_ref.1, s32[96]{0:T(128)} %tile_ref.1, s32[16384]{0:T(1024)} %owner_ref.1, f32[512,128]{1,0:T(8,128)} %jones_ref.1), custom_call_target="tpu_custom_call" | custom-call | flops 10000000 | bytes 500000 | tf_op jit(solution)/shard_map/prep/pallas_call | solution.py:347
  7.8 0.0 copy-start.5
  7.8 0.9 %copy-done.5 = f32[24,2,2,16,128]{4,3,2,1,0:T(8,128)} copy-done((f32[24,2,2,16,128]{4,3,2,1,0:T(8,128)}, f32[24,2,2,16,128]{4,3,2,1,0:T(8,128)S(1)}, u32[]{:S(2)}) %copy-start.5) | copy-done | bytes 786456
  8.7 12.5 %grid_chunk.3 = (f32[24,16,128]{2,1,0:T(8,128)}, f32[24,16,128]{2,1,0:T(8,128)}) custom-call(s32[1]{0:T(128)} %bitcast.section_ref.refs_0_, f32[96]{0:T(128)} %refs_1_.3, f32[16,16,128]{2,1,0:T(8,128)} %get-tuple-element.14.refs_2_, f32[1,96,2,2,16,128]{5,4,3,2,1,0:T(8,128)} %refs_3_.3, f32[24,2,2,16,128]{4,3,2,1,0:T(8,128)} %copy-done.5, ...), custom_call_target="tpu_custom_call" | custom-call | flops 7200000000 | bytes 2400000 | tf_op jit(solution)/shard_map/grid_chunk/pallas_call | solution.py:370
  21.2 0.2 collective-permute-start.3
  21.4 0.9 %copy-done.4 = f32[24,2,2,16,128]{4,3,2,1,0:T(8,128)} copy-done((f32[24,2,2,16,128]{4,3,2,1,0:T(8,128)}, f32[24,2,2,16,128]{4,3,2,1,0:T(8,128)S(1)}, u32[]{:S(2)}) %copy-start.4) | copy-done | bytes 786456
  22.3 12.5 %grid_chunk.2 = (f32[24,16,128]{2,1,0:T(8,128)}, f32[24,16,128]{2,1,0:T(8,128)}) custom-call(s32[1]{0:T(128)} %bitcast.section_ref.refs_0_, f32[96]{0:T(128)} %refs_1_.3, f32[16,16,128]{2,1,0:T(8,128)} %get-tuple-element.14.refs_2_, f32[1,96,2,2,16,128]{5,4,3,2,1,0:T(8,128)} %refs_3_.3, f32[24,2,2,16,128]{4,3,2,1,0:T(8,128)} %copy-done.4, ...), custom_call_target="tpu_custom_call" | custom-call | flops 7200000000 | bytes 2400000 | tf_op jit(solution)/shard_map/grid_chunk/pallas_call | solution.py:370
  34.8 0.4 collective-permute-start.2
  35.2 0.7 all_to_all.9
  35.9 11.5 %all-to-all-start = ((s32[64,1,2]{2,1,0:T(1,128)}), s32[64,1,2]{2,1,0:T(1,128)S(1)}, u32[]{:S(2)}, u32[]{:S(2)}) async-start(s32[64,1,2]{2,1,0:T(1,128)} %bitcast.1), calls=%async_computation | async-start | bytes 65536 | tf_op jit(solution)/shard_map/all_to_all | solution.py:415
  47.5 0.7 copy-done.1
  48.1 0.1 copy-done.2
  48.2 2.9 %pack.1 = f32[128,16,128]{2,1,0:T(8,128)} custom-call(s32[1]{0:T(128)} %bitcast.section_ref.refs_0_, s32[96]{0:T(128)} %get-tuple-element.13.row_ref, f32[24,16,128]{2,1,0:T(8,128)} %get-tuple-element.15.refs_0_, f32[24,16,128]{2,1,0:T(8,128)} %get-tuple-element.16.refs_1_, f32[24,16,128]{2,1,0:T(8,128)} %copy-done.2, f32[24,16,128]{2,1,0:T(8,128)} %copy-done.1), custom_call_target="tpu_custom_call" | custom-call | tf_op jit(solution)/shard_map/pack/pallas_call | solution.py:428
  51.1 5.9 %all-to-all-done = s32[64,1,2]{2,1,0:T(1,128)S(1)} async-done(((s32[64,1,2]{2,1,0:T(1,128)}), s32[64,1,2]{2,1,0:T(1,128)S(1)}, u32[]{:S(2)}, u32[]{:S(2)}) %all-to-all-start) | async-done | bytes 544 | tf_op jit(solution)/shard_map/all_to_all | solution.py:415
  57.0 5.0 %all-to-all-start.1 = ((f32[64,2,16,128]{3,2,1,0:T(8,128)}), f32[64,2,16,128]{3,2,1,0:T(8,128)S(1)}, u32[]{:S(2)}, u32[]{:S(2)}) async-start(f32[64,2,16,128]{3,2,1,0:T(8,128)} %bitcast.9), calls=%async_computation.1 | async-start | bytes 2097152 | tf_op jit(solution)/shard_map/all_to_all | solution.py:435
  62.0 0.6 broadcast.3
  62.6 0.7 reduce.3
  63.3 0.7 reshape.20.slot_ref
  64.0 16.0 %all-to-all-done.1 = f32[64,2,16,128]{3,2,1,0:T(8,128)S(1)} async-done(((f32[64,2,16,128]{3,2,1,0:T(8,128)}), f32[64,2,16,128]{3,2,1,0:T(8,128)S(1)}, u32[]{:S(2)}, u32[]{:S(2)}) %all-to-all-start.1) | async-done | bytes 1048608 | tf_op jit(solution)/shard_map/all_to_all | solution.py:435
  79.9 1.0 %copy-done = f32[64,2,16,128]{3,2,1,0:T(8,128)} copy-done((f32[64,2,16,128]{3,2,1,0:T(8,128)}, f32[64,2,16,128]{3,2,1,0:T(8,128)S(1)}, u32[]{:S(2)}) %copy-start) | copy-done | bytes 1048600
  80.9 4.5 %unpack.1 = f32[256,2048]{1,0:T(8,128)} custom-call(s32[128]{0:T(128)} %reshape.20.slot_ref, f32[128,16,128]{2,1,0:T(8,128)} %bitcast.10), custom_call_target="tpu_custom_call" | custom-call | tf_op jit(solution)/shard_map/unpack/pallas_call | solution.py:438
  (10 shorter events, 0.0 us)
Async XLA Ops:
  1.5 6.3 %collective-permute-start.1 = (f32[24,2,2,16,128]{4,3,2,1,0:T(8,128)S(1)}, f32[24,2,2,16,128]{4,3,2,1,0:T(8,128)S(1)}, u32[]{:S(2)}, u32[]{:S(2)}) collective-permute-start(f32[24,2,2,16,128]{4,3,2,1,0:T(8,128)S(1)} %get-tuple-element.19), channel_id=1, source_target_pairs={{0,64},{64,0},{1,65},{65,1},{2,66},{66,2},{3,67},{67,3},{4,68},{68... | collective-permute-start | bytes 2359304 | tf_op jit(solution)/shard_map/ppermute | solution.py:412
  1.6 19.8 %collective-permute-start = (f32[24,2,2,16,128]{4,3,2,1,0:T(8,128)S(1)}, f32[24,2,2,16,128]{4,3,2,1,0:T(8,128)S(1)}, u32[]{:S(2)}, u32[]{:S(2)}) collective-permute-start(f32[24,2,2,16,128]{4,3,2,1,0:T(8,128)S(1)} %get-tuple-element.20), channel_id=1, source_target_pairs={{0,64},{64,0},{1,65},{65,1},{2,66},{66,2},{3,67},{67,3},{4,68},{68... | collective-permute-start | bytes 2359304 | tf_op jit(solution)/shard_map/ppermute | solution.py:412
  7.8 0.9 %copy-start.5 = (f32[24,2,2,16,128]{4,3,2,1,0:T(8,128)}, f32[24,2,2,16,128]{4,3,2,1,0:T(8,128)S(1)}, u32[]{:S(2)}) copy-start(f32[24,2,2,16,128]{4,3,2,1,0:T(8,128)S(1)} %collective-permute-done.1.refs_4_) | copy-start | bytes 2359300
  21.2 14.0 %copy-start.3 = (s32[128]{0:T(128)S(1)}, s32[128]{0:T(128)}, u32[]{:S(2)}) copy-start(s32[128]{0:T(128)} %get-tuple-element.12) | copy-start | bytes 1540
  21.2 26.2 %collective-permute-start.3 = (f32[24,16,128]{2,1,0:T(8,128)}, f32[24,16,128]{2,1,0:T(8,128)S(1)}, u32[]{:S(2)}, u32[]{:S(2)}) collective-permute-start(f32[24,16,128]{2,1,0:T(8,128)} %get-tuple-element.18), channel_id=1, source_target_pairs={{0,64},{64,0},{1,65},{65,1},{2,66},{66,2},{3,67},{67,3},{4,68},{68... | collective-permute-start | bytes 589832 | tf_op jit(solution)/shard_map/ppermute | solution.py:426
  21.4 0.9 %copy-start.4 = (f32[24,2,2,16,128]{4,3,2,1,0:T(8,128)}, f32[24,2,2,16,128]{4,3,2,1,0:T(8,128)S(1)}, u32[]{:S(2)}) copy-start(f32[24,2,2,16,128]{4,3,2,1,0:T(8,128)S(1)} %collective-permute-done.refs_4_) | copy-start | bytes 2359300
  34.8 12.7 %collective-permute-start.2 = (f32[24,16,128]{2,1,0:T(8,128)}, f32[24,16,128]{2,1,0:T(8,128)S(1)}, u32[]{:S(2)}, u32[]{:S(2)}) collective-permute-start(f32[24,16,128]{2,1,0:T(8,128)} %get-tuple-element.17), channel_id=1, source_target_pairs={{0,64},{64,0},{1,65},{65,1},{2,66},{66,2},{3,67},{67,3},{4,68},{68... | collective-permute-start | bytes 589832 | tf_op jit(solution)/shard_map/ppermute | solution.py:426
  35.9 21.1 %all-to-all-start = ((s32[64,1,2]{2,1,0:T(1,128)}), s32[64,1,2]{2,1,0:T(1,128)S(1)}, u32[]{:S(2)}, u32[]{:S(2)}) async-start(s32[64,1,2]{2,1,0:T(1,128)} %bitcast.1), calls=%async_computation | async-start | bytes 65536 | tf_op jit(solution)/shard_map/all_to_all | solution.py:415
  47.4 0.7 copy-start.1
  47.5 0.7 copy-start.2
  57.0 22.9 %all-to-all-start.1 = ((f32[64,2,16,128]{3,2,1,0:T(8,128)}), f32[64,2,16,128]{3,2,1,0:T(8,128)S(1)}, u32[]{:S(2)}, u32[]{:S(2)}) async-start(f32[64,2,16,128]{3,2,1,0:T(8,128)} %bitcast.9), calls=%async_computation.1 | async-start | bytes 2097152 | tf_op jit(solution)/shard_map/all_to_all | solution.py:435
  79.9 1.0 %copy-start = (f32[64,2,16,128]{3,2,1,0:T(8,128)}, f32[64,2,16,128]{3,2,1,0:T(8,128)S(1)}, u32[]{:S(2)}) copy-start(f32[64,2,16,128]{3,2,1,0:T(8,128)S(1)} %all-to-all-done.1) | copy-start | bytes 3145732

commit v2 on v0

v2 whole, which is shorter than its diff:
```python
import math

import numpy as np
import jax
import jax.numpy as jnp
from jax import lax
from jax.experimental import pallas as pl
from jax.experimental.pallas import tpu as pltpu
from jax.sharding import PartitionSpec as P

SIDE = 32
CHUNKS = (48,)
GROUP = 4

PIXELS = np.concatenate([np.arange(16), -1 - np.arange(16)]).astype(np.float64)


def fit_even(function, reach, terms):
    nodes = np.cos(np.pi * (np.arange(64) + 0.5) / 64)
    square = (nodes + 1.0) / 2.0 * reach * reach
    cheb = np.polynomial.chebyshev.chebfit(nodes, function(np.sqrt(square)), terms - 1)
    poly = np.polynomial.chebyshev.cheb2poly(cheb)
    shift = np.polynomial.polynomial.Polynomial(poly)(
        np.polynomial.polynomial.Polynomial([-1.0, 2.0 / (reach * reach)])
    )
    return [float(np.float32(value)) for value in shift.coef]


def sinc_turns(scale):
    return lambda x: np.where(x > 0, np.sin(scale * x) / np.maximum(x, 1e-30), scale)


HALF_SIN = fit_even(sinc_turns(np.pi), 0.5, 5)
HALF_COS = fit_even(lambda x: np.cos(np.pi * x), 0.5, 6)
STEP_SIN = fit_even(sinc_turns(2 * np.pi), 0.0625, 3)
STEP_COS = fit_even(lambda x: np.cos(2 * np.pi * x), 0.0625, 4)


def horner(coefs, square):
    total = square * coefs[-1] + coefs[-2]
    for value in coefs[-3::-1]:
        total = total * square + value
    return total


def sincos_half(x):
    square = x * x
    half_sin = x * horner(HALF_SIN, square)
    half_cos = horner(HALF_COS, square)
    twice = half_sin + half_sin
    return twice * half_cos, 1.0 - twice * half_sin


def sincos_turns(x):
    return sincos_half(x - jnp.round(x))


def sincos_step(x):
    square = x * x
    return x * horner(STEP_SIN, square), horner(STEP_COS, square)


def spread(ref, row):
    return ref[pl.ds(row, 8, stride=0), :]


def split_hi_lo(values):
    high = values.astype(jnp.bfloat16)
    low = (values - high.astype(jnp.float32)).astype(jnp.bfloat16)
    return high, low


def np_split(values):
    high = np.asarray(values, np.float32).astype(jnp.bfloat16)
    low = (np.asarray(values, np.float32) - high.astype(np.float32)).astype(jnp.bfloat16)
    return high, low


def tables(samples):
    row_p = PIXELS[:, None]
    lane_p = np.tile(PIXELS, GROUP)[None, :]
    sine_row, sine_lane = 0.6 * row_p / SIDE, 0.6 * lane_p / SIDE
    n_term = np.sqrt(1.0 - sine_row**2 - sine_lane**2) - 1.0
    taper = np.cos(np.pi * row_p / (SIDE + 4.0)) * np.cos(np.pi * lane_p / (SIDE + 4.0))
    pixel_tables = np.stack([n_term, taper / math.sqrt(samples) / SIDE]).astype(np.float32)

    freq = np.arange(SIDE) - SIDE // 2
    angle = 2.0 * np.pi / SIDE * PIXELS[:, None] * freq[None, :]
    cos_t = np.kron(np.eye(GROUP), np.cos(angle))
    sin_t = np.kron(np.eye(GROUP), np.sin(angle))
    high, low = np_split(np.block([[cos_t, -sin_t], [sin_t, cos_t]]))
    right_all = np.concatenate([high, high, low], 0)

    order = np.arange(SIDE).reshape(8, 4).T.reshape(-1)
    angle = 2.0 * np.pi / SIDE * freq[order][:, None] * PIXELS[None, :]
    high, low = np_split(np.block([[np.cos(angle), np.sin(angle)], [-np.sin(angle), np.cos(angle)]]))
    left_all = np.concatenate([high, high, low], 1)
    return pixel_tables, right_all, left_all


def swap_groups(parts, low_half, odd_quarter):
    a0 = jnp.where(low_half, parts[0], pltpu.roll(parts[2], 64, 1))
    a2 = jnp.where(low_half, pltpu.roll(parts[0], 64, 1), parts[2])
    a1 = jnp.where(low_half, parts[1], pltpu.roll(parts[3], 64, 1))
    a3 = jnp.where(low_half, pltpu.roll(parts[1], 64, 1), parts[3])
    return [
        jnp.where(odd_quarter, pltpu.roll(a1, 32, 1), a0),
        jnp.where(odd_quarter, a1, pltpu.roll(a0, 96, 1)),
        jnp.where(odd_quarter, pltpu.roll(a3, 32, 1), a2),
        jnp.where(odd_quarter, a3, pltpu.roll(a2, 96, 1)),
    ]


def gains_kernel(section_ref, stations_ref, jones_ref, coef_ref, p_rows, q_rows, turned):
    section = section_ref[0]
    half = stations_ref.shape[1] // 2
    p_rows[...] = jnp.zeros_like(p_rows)
    q_rows[...] = jnp.zeros_like(q_rows)

    def fetch(step, carry):
        for k in range(8):
            item = section * half + step * 8 + k
            p_rows[pl.ds(step * 8 + k, 1), :] = jones_ref[pl.ds(stations_ref[0, item], 1), :]
            q_rows[pl.ds(step * 8 + k, 1), :] = jones_ref[pl.ds(stations_ref[1, item], 1), :]
        return carry

    lax.fori_loop(0, half // 8, fetch, 0)
    lane = lax.broadcasted_iota(jnp.int32, (128, 128), 1)
    odd = (lane & 1) == 1
    high_pair = (lane & 2) == 2

    def swap_one(x):
        return jnp.where(odd, pltpu.roll(x, 1, 1), pltpu.roll(x, 127, 1))

    def swap_two(x):
        return jnp.where(high_pair, pltpu.roll(x, 2, 1), pltpu.roll(x, 126, 1))

    gain_p = p_rows[...]
    gain_p_turned = swap_one(gain_p)
    for kind in range(2):
        gain_q = q_rows[...] if kind == 0 else swap_two(q_rows[...])
        straight = gain_p * gain_q
        crossed = gain_p_turned * gain_q
        real = straight + swap_one(straight)
        imag = swap_one(crossed) - crossed
        turned[...] = jnp.where(odd, imag, real).T
        for place in range(8):
            coef_ref[kind * 8 + place] = turned[pl.ds(place, 16, stride=8), :]


def index_kernel(tile_ref, owner_ref, row_ref, slot_ref):
    sub_count = tile_ref.shape[0]
    tiles_dev = owner_ref.shape[0] // (slot_ref.shape[0] // 2)
    shift = tiles_dev.bit_length() - 1
    assert tiles_dev == 1 << shift

    def clear(step, carry):
        for k in range(4):
            slot_ref[step * 4 + k] = -1
        return carry

    lax.fori_loop(0, slot_ref.shape[0] // 4, clear, 0)

    def place_item(step, carry):
        for k in range(8):
            item = step * 8 + k
            position = owner_ref[tile_ref[item]]
            target = 2 * (position >> shift)
            slot = position & (tiles_dev - 1)
            first = slot_ref[target]
            row = target + jnp.where((first == -1) | (first == slot), 0, 1)
            slot_ref[row] = slot
            row_ref[item] = row
        return carry

    lax.fori_loop(0, sub_count // 8, place_item, 0)


def grid_kernel(chunk_start, section_ref, w_ref, coef_ref, own_ref, peer_ref, uv_ref, pixel_ref, right_ref, left_ref,
                mine_ref, other_ref, bcast, rolled, wave_rows, totals):
    section = section_ref[0]
    groups = mine_ref.shape[0] // GROUP
    half = w_ref.shape[0] // 2
    lane = lax.broadcasted_iota(jnp.int32, (8, 128), 1)
    sub_lane = lax.broadcasted_iota(jnp.int32, (8, 128), 0).astype(jnp.float32)

    def gridding(group):
        first = group * GROUP
        shift = lax.rem(128 - (chunk_start + first), 128)
        for place in range(16):
            rolled[place] = pltpu.roll(coef_ref[place], shift, 1)
        cells = uv_ref[pl.ds(pl.multiple_of(section * (2 * half) + 2 * (chunk_start + first), 8), 8), :]
        wave_rows[0:8], wave_rows[8:16] = sincos_turns(cells * (8.0 / SIDE))
        wave_rows[16:24], wave_rows[24:32] = sincos_step(cells * (8.0 / (64.0 * SIDE)))
        sums = cells + pltpu.roll(cells, 7, 0)
        wave_rows[32:40], wave_rows[40:48] = sincos_step(sums * (8.0 / (128.0 * SIDE)))
        wave_rows[48:56] = cells
        for g in range(GROUP):
            corr = [None, None]
            for row in range(2):
                for kind in range(2):
                    column = (row ^ section) ^ kind
                    source = own_ref if row == 0 else peer_ref
                    vis_real = source[first + g, column, 0]
                    vis_imag = source[first + g, column, 1]
                    for pol in range(2):
                        place = kind * 8 + (pol ^ section) * 4 + (row ^ section) * 2
                        cr = jnp.broadcast_to(rolled[place][:, g : g + 1], (16, 128))
                        ci = jnp.broadcast_to(rolled[place + 1][:, g : g + 1], (16, 128))
                        real = cr * vis_real - ci * vis_imag
                        imag = cr * vis_imag + ci * vis_real
                        if corr[pol] is None:
                            corr[pol] = [real, imag]
                        else:
                            corr[pol] = [corr[pol][0] + real, corr[pol][1] + imag]
            u_row = spread(wave_rows, 48 + 2 * g)
            v_row = spread(wave_rows, 49 + 2 * g)
            turn_sin, turn_cos = sincos_half((u_row + v_row) * ((1.0 + sub_lane / 64.0) / (2.0 * SIDE)))
            step_sin, step_cos = spread(wave_rows, 32 + 2 * g), spread(wave_rows, 40 + 2 * g)
            turn_sin, turn_cos = (
                jnp.concatenate([turn_sin, turn_sin * step_cos + turn_cos * step_sin], 0),
                jnp.concatenate([turn_cos, turn_cos * step_cos - turn_sin * step_sin], 0),
            )
            for pol in range(2):
                real, imag = corr[pol]
                bcast[g, pol * 16 : pol * 16 + 16] = real * turn_cos + imag * turn_sin
                bcast[g, 32 + pol * 16 : 48 + pol * 16] = imag * turn_cos - real * turn_sin

            waves = []
            for axis, cell in enumerate((u_row, v_row)):
                turns = cell * ((sub_lane + 0.5) / SIDE)
                sin_0, cos_0 = sincos_turns(turns)
                sin_d, cos_d = sincos_step(turns * (1.0 / 64.0))
                place = 2 * g + axis
                up_sin, up_cos = spread(wave_rows, place), spread(wave_rows, 8 + place)
                upd_sin, upd_cos = spread(wave_rows, 16 + place), spread(wave_rows, 24 + place)
                cos_0, sin_0, cos_d, sin_d = (
                    jnp.stack([cos_0, cos_0 * up_cos - sin_0 * up_sin]),
                    jnp.stack([sin_0, sin_0 * up_cos + cos_0 * up_sin]),
                    jnp.stack([cos_d, cos_d * upd_cos - sin_d * upd_sin]),
                    jnp.stack([sin_d, sin_d * upd_cos + cos_d * upd_sin]),
                )
                cos_1 = cos_0 * cos_d - sin_0 * sin_d
                sin_1 = sin_0 * cos_d + cos_0 * sin_d
                waves.append([cos_0, sin_0, cos_1, sin_1, cos_d + cos_d])
            total = None
            for pair in range(8):
                left_parts, right_parts = [], []
                for c in (2 * pair, 2 * pair + 1):
                    cos_u, sin_u = waves[0][0], waves[0][1]
                    cos_v, sin_v = waves[1][0], waves[1][1]
                    left_parts.append(jnp.concatenate([cos_u, sin_u], 0).reshape(32, 128))
                    pieces = []
                    for k in range(4):
                        line = spread(bcast.at[g], 16 * k + c)[None]
                        pieces.append((cos_v * line).reshape(16, 128))
                        pieces.append((sin_v * line).reshape(16, 128))
                    right_parts.append(jnp.concatenate(pieces, 0))
                    for wave in waves:
                        cos_0, sin_0, cos_1, sin_1, twice = wave
                        wave[0], wave[1] = cos_1, sin_1
                        if c < 14:
                            wave[2], wave[3] = twice * cos_1 - cos_0, twice * sin_1 - sin_0
                part = lax.dot_general(
                    jnp.concatenate(left_parts, 1).astype(jnp.bfloat16),
                    jnp.concatenate(right_parts, 1).astype(jnp.bfloat16),
                    (((1,), (1,)), ((), ())),
                    preferred_element_type=jnp.float32,
                )
                total = part if total is None else total + part
            totals[group & 1, g] = total

    def imaging(group):
        first = group * GROUP
        lane32 = lax.broadcasted_iota(jnp.int32, (32, 128), 1)
        lane16 = lax.broadcasted_iota(jnp.int32, (16, 128), 1)
        sums = swap_groups(
            [totals[group & 1, g] for g in range(GROUP)], lane32 < 64, (lane32 & 32) == 32
        )
        upper = (lane16 & 16) == 16
        sign = jnp.where(upper, -1.0, 1.0)
        w_first = section * half + chunk_start + first
        w_row = jnp.where(
            lane < 64,
            jnp.where(lane < 32, w_ref[w_first], w_ref[w_first + 1]),
            jnp.where(lane < 96, w_ref[w_first + 2], w_ref[w_first + 3]),
        )
        w_turns = pixel_ref[0].reshape(4, 8, 128) * w_row[None]
        w_sin, w_cos = sincos_turns(w_turns.reshape(32, 128))
        w_sin, w_cos = w_sin * pixel_ref[1], w_cos * pixel_ref[1]
        fields = []
        for pol in range(2):
            cos_part, sin_part = [], []
            for value in (sums[pol][:16], sums[2 + pol][:16], sums[pol][16:], sums[2 + pol][16:]):
                cos_part.append(jnp.where(upper, pltpu.roll(value, 16, 1), value))
                sin_part.append(sign * jnp.where(upper, value, pltpu.roll(value, 112, 1)))
            even_re = cos_part[0] - sin_part[1]
            even_im = cos_part[1] + sin_part[0]
            odd_re = cos_part[3] + sin_part[2]
            odd_im = cos_part[2] - sin_part[3]
            image_re = jnp.concatenate([even_re - odd_re, even_re + odd_re], 0)
            image_im = jnp.concatenate([even_im + odd_im, even_im - odd_im], 0)
            fields.append(
                jnp.concatenate(
                    [image_re * w_cos - image_im * w_sin, image_re * w_sin + image_im * w_cos], 1
                )
            )
        high, low = split_hi_lo(jnp.concatenate(fields, 0))
        rows = jnp.dot(
            jnp.concatenate([high, low, high], 1), right_ref[...], preferred_element_type=jnp.float32
        )
        high, low = split_hi_lo(rows)
        for pol, out_ref in enumerate((mine_ref, other_ref)):
            top = slice(pol * 32, pol * 32 + 32)
            stack = jnp.concatenate(
                [high[top, :128], high[top, 128:], low[top, :128], low[top, 128:], high[top, :128], high[top, 128:]],
                0,
            )
            uv = jnp.dot(left_ref[...], stack, preferred_element_type=jnp.float32)
            for part in range(2):
                parts = swap_groups(
                    [uv[part * 32 + k * 8 : part * 32 + k * 8 + 8] for k in range(4)], lane < 64, (lane & 32) == 32
                )
                for g in range(GROUP):
                    out_ref[first + g, part * 8 : part * 8 + 8, :] = parts[g]

    gridding(0)

    def both(group, carry):
        imaging(group - 1)
        gridding(group)
        return carry

    lax.fori_loop(1, groups, both, 0)
    imaging(groups - 1)


def pack_kernel(section_ref, row_ref, slot_ref, *refs):
    packed = refs[-1]
    section = section_ref[0]
    half = row_ref.shape[0] // 2
    width = packed.shape[0] // (slot_ref.shape[0] // 2)
    packed[...] = jnp.zeros_like(packed)
    lane = lax.broadcasted_iota(jnp.int32, (1, 128), 1)

    def note(step, carry):
        for k in range(2):
            target = step * 2 + k
            slots = jnp.where(lane == 0, slot_ref[2 * target], slot_ref[2 * target + 1])
            packed[pl.ds(target * width + width - 1, 1), :] = slots.astype(jnp.float32)
        return carry

    lax.fori_loop(0, slot_ref.shape[0] // 4, note, 0)
    add_rows(row_ref, section * half, width, refs[:-1], packed)


def pack_more_kernel(section_ref, row_ref, *refs):
    packed = refs[-1]
    half = row_ref.shape[0] // 2
    packed[...] = refs[0][...]
    add_rows(row_ref, (1 - section_ref[0]) * half, 33, refs[1:-1], packed)


def add_rows(row_ref, start, width, sources, packed):
    for values in sources:

        def add(step, carry, values=values, start=start):
            for k in range(4):
                item = step * 4 + k
                row = row_ref[start + item]
                top = (row >> 1) * width + (row & 1) * 16
                packed[pl.ds(top, 16), :] = packed[pl.ds(top, 16), :] + values[item]
            return carry

        lax.fori_loop(0, values.shape[0] // 4, add, 0)
        start = start + values.shape[0]


def unpack_kernel(received_ref, out_ref):
    tiles_dev = out_ref.shape[0]
    sources = received_ref.shape[0] // 33
    slots = received_ref[pl.ds(32, sources, stride=33), :].T
    row = jnp.concatenate([slots[0:1, :], slots[1:2, :]], 1)
    tile = lax.broadcasted_iota(jnp.int32, (tiles_dev, 2 * sources), 0).astype(jnp.float32)
    picked = jnp.where(tile == row, 1.0, 0.0).astype(jnp.bfloat16)
    picked = jnp.concatenate([picked, picked], 1)
    for pair in range(8):
        columns = []
        for column in (2 * pair, 2 * pair + 1):
            values = jnp.concatenate(
                [received_ref[pl.ds(16 * rank + column, sources, stride=33), :] for rank in range(2)], 0
            )
            columns.append(jnp.concatenate(split_hi_lo(values), 0))
        out_ref[:, pair * 256 : (pair + 1) * 256] = jnp.dot(
            picked, jnp.concatenate(columns, 1), preferred_element_type=jnp.float32
        )


SMEM = pl.BlockSpec(memory_space=pltpu.SMEM)
VMEM = pl.BlockSpec(memory_space=pltpu.VMEM)


def call(kernel, name, out_shape, in_specs, out_specs, scratch=(), flops=1_000_000, moved=1_000_000, mib=8):
    return pl.pallas_call(
        kernel,
        out_shape=out_shape,
        in_specs=in_specs,
        out_specs=out_specs,
        scratch_shapes=list(scratch),
        compiler_params=pltpu.CompilerParams(vmem_limit_bytes=mib * 1024 * 1024),
        cost_estimate=pl.CostEstimate(flops=flops, bytes_accessed=moved, transcendentals=0),
        name=name,
    )


def shards(visibilities, uv_coords, w_terms, stations, tile_ids, owner_map, jones_gains):
    sub_count = visibilities.shape[1]
    samples = visibilities.shape[4] * visibilities.shape[5]
    half = sub_count // 2
    grid_size = lax.axis_size("grid")
    tiles_dev = owner_map.shape[0] // grid_size
    section_index = lax.axis_index("section").astype(jnp.int32)
    section = section_index.reshape(1)
    swap = [(0, 1), (1, 0)]
    shape_f32 = lambda *shape: jax.ShapeDtypeStruct(shape, jnp.float32)
    shape_i32 = lambda *shape: jax.ShapeDtypeStruct(shape, jnp.int32)

    own, peers, start = [], [], 0
    for size in CHUNKS:
        rows = lax.dynamic_slice_in_dim(visibilities[0], (1 - section_index) * half + start, size, 0)
        peers.append(lax.ppermute(rows, "section", swap))
        start += size
    start = 0
    for size in CHUNKS:
        own.append(lax.dynamic_slice_in_dim(visibilities[0], section_index * half + start, size, 0))
        start += size

    coefs = call(
        gains_kernel, "gains", shape_f32(16, 16, 128), [SMEM, SMEM, VMEM], VMEM,
        [pltpu.VMEM((128, 128), jnp.float32)] * 3,
    )(section, stations, jones_gains)
    row_index, slots = call(
        index_kernel, "index", (shape_i32(sub_count), shape_i32(2 * grid_size)), [SMEM, SMEM], (SMEM, SMEM)
    )(tile_ids, owner_map)

    constants = [jnp.asarray(table) for table in tables(samples)]
    uv_rows = uv_coords.reshape(2 * sub_count, uv_coords.shape[2])
    mine, theirs, start = [], [], 0
    for chunk, size in enumerate(CHUNKS):
        kept, other = call(
            lambda *refs, start=start: grid_kernel(start, *refs),
            "grid_chunk",
            (shape_f32(size, 16, 128),) * 2,
            [SMEM, SMEM] + [VMEM] * 7,
            (VMEM, VMEM),
            [
                pltpu.VMEM((GROUP, 64, 128), jnp.float32),
                pltpu.VMEM((16, 16, 128), jnp.float32),
                pltpu.VMEM((56, 128), jnp.float32),
                pltpu.VMEM((2, GROUP, 32, 128), jnp.float32),
            ],
            flops=size * 300_000_000,
            moved=size * 100_000,
            mib=12,
        )(section, w_terms, coefs, own[chunk], peers[chunk], uv_rows, *constants)
        mine.append(kept)
        theirs.append(lax.ppermute(other, "section", swap))
        start += size

    packed_shape = shape_f32(33 * grid_size, 128)
    packed = call(
        pack_kernel, "pack", packed_shape, [SMEM] * 3 + [VMEM] * len(CHUNKS), VMEM, flops=100_000_000
    )(section, row_index, slots, *mine)
    packed = call(
        pack_more_kernel, "pack_more", packed_shape, [SMEM] * 2 + [VMEM] * (1 + len(CHUNKS)), VMEM
    )(section, row_index, packed, *theirs)
    received = lax.all_to_all(
        packed.reshape(grid_size, 1, 33 * 128), "grid", split_axis=0, concat_axis=0, tiled=True
    ).reshape(33 * grid_size, 128)
    tiles = call(unpack_kernel, "unpack", shape_f32(tiles_dev, 2048), [VMEM], VMEM)(received)
    return tiles[None]


def solution(mesh):
    in_specs = (
        P("section", "grid", None, None, None, None),
        P("grid", None, None),
        P("grid"),
        P(None, "grid"),
        P("grid"),
        P(),
        P(),
    )
    out_specs = P("section", "grid", None)
    return jax.shard_map(shards, mesh=mesh, in_specs=in_specs, out_specs=out_specs, check_vma=False)
```

time: 780 us -> 59.5 us (0.08)
  blocking collectives: 350 us -> 30.9 us
  other arithmetic: 229 us -> 0 us
  local copies, waits for them, and re-layouts: 155 us -> 2.33 us
  matrix products: 38.7 us -> 0 us
  Pallas kernels: 0 us -> 23.5 us
    unnamed x1 -> x0, blocking collectives: 350 us -> none
    sin x3 -> x0, other arithmetic: 181 us -> none  [subgrid_tiles(): wave_imag = jnp.sin(phase_angle)]
    gather x5 -> x0, local copies, waits for them, and re-layouts: 75.6 us -> none  [the longest x3 41.3 us: lead_ranks(): return place_rank[leader]]
    dot_general x28 -> x0, matrix products: 38.7 us -> none  [the longest x3 17.8 us: subgrid_tiles(): jnp.einsum('nxk,nyk->nxy', weighted, basis, preferred_element_type=jnp.fl...]
    all_to_all x0 -> x1, blocking collectives: none -> 30.9 us  [shards(): lax.all_to_all(packed.reshape(grid_size, 1, 33 * 128), 'grid', split_axis...]
    squeeze x15 -> x0, local copies, waits for them, and re-layouts: 25.9 us -> none  [the longest x3 18.6 us: subgrid_tiles(): wave_real[:, 1]]
    pallas_call x0 -> x6, Pallas kernels: none -> 23.5 us  [the longest x1 15.3 us: shards(): call(lambda *refs, start=start: grid_kernel(start, *refs), 'grid_chunk',...]
    another operation x4 -> x0, other arithmetic: 23.3 us -> none
  transfers between devices with their start and end apart: 2 -> 2, of which waited for: 0 -> 1; matrix products, arithmetic and copies ran while one was open for 16% -> 0% of each run, Pallas kernels for 0% -> 9%
where the time goes in v2:
time: 59.5 us; the launch traced here: 59.4 us
  blocking collectives  30.9 us (52%)
  Pallas kernels  23.5 us (39%)
  local copies, waits for them, and re-layouts  2.33 us (4%)
  waiting for transfers between devices  2.24 us (4%)
    all_to_all x1, blocking collectives, shards(): lax.all_to_all(packed.reshape(grid_size, 1, 33 * 128), 'grid', split_axis...  30.9 us
    pallas_call x1, Pallas kernels, shards(): call(lambda *refs, start=start: grid_kernel(start, *refs), 'grid_chunk',...  15.3 us
    pallas_call x1, Pallas kernels, shards(): call(index_kernel, 'index', (shape_i32(sub_count), shape_i32(2 * grid_siz...  3.26 us
    dynamic_slice x1, local copies, waits for them, and re-layouts, shards(): lax.dynamic_slice_in_dim(visibilities[0], (1 - section_index) * half + st...  2.29 us
    ppermute x1, waiting for transfers between devices, shards(): peers.append(lax.ppermute(rows, 'section', swap))  2.24 us
    pallas_call x1, Pallas kernels, shards(): call(unpack_kernel, 'unpack', shape_f32(tiles_dev, 2048), [VMEM], VMEM)  1.87 us
  transfers between devices with their start and end apart: 2, of which 1 were waited for; matrix products, arithmetic and copies ran while one was open for 0% of the time, Pallas kernels for 9%

profile of v2, /device:TPU:0, one launch (start us, length us, event | category | flops | bytes accessed | tf_op | source)
XLA Modules:
  0.0 59.4 jit_solution(14114686275643678077)
XLA Ops:
  0.0 0.0 copy-start.7
  0.0 0.0 copy-start.8
  0.0 2.3 %dynamic-slice_bitcast_fusion = (f32[48,2,2,16,128]{4,3,2,1,0:T(8,128)S(1)}, f32[48,2,2,16,128]{4,3,2,1,0:T(8,128)S(1)}) fusion(f32[1,96,2,2,16,128]{5,4,3,2,1,0:T(8,128)} %param.10, s32[]{:T(128)S(6)} %select_n.7, s32[]{:T(128)S(6)} %select_n.6), kind=kLoop, calls=%fused_computation | loop fusion | bytes 6291464 | tf_op jit(solution)/shard_map/dynamic_slice | solution.py:430
  2.3 0.1 collective-permute-start
  2.4 0.0 copy-done
  2.4 0.0 copy-done.2
  2.4 1.1 %gains.1.refs_2_ = f32[16,16,128]{2,1,0:T(8,128)S(1)} custom-call(s32[1]{0:T(128)} %bitcast.section_ref.refs_0_, s32[2,96]{1,0:T(2,128)S(1)} %copy-done.2, f32[512,128]{1,0:T(8,128)S(1)} %copy-done), custom_call_target="tpu_custom_call" | custom-call | flops 1000000 | bytes 1000000 | tf_op jit(solution)/shard_map/gains/pallas_call | solution.py:438
  3.6 2.2 %collective-permute-done.refs_4_ = f32[48,2,2,16,128]{4,3,2,1,0:T(8,128)S(1)} collective-permute-done((f32[48,2,2,16,128]{4,3,2,1,0:T(8,128)S(1)}, f32[48,2,2,16,128]{4,3,2,1,0:T(8,128)S(1)}, u32[]{:S(2)}, u32[]{:S(2)}) %collective-permute-start) | collective-permute-done | bytes 1572896 | tf_op jit(solution)/shard_map/ppermute | solution.py:431
  5.8 0.0 copy-done.4
  5.8 0.0 copy-done.5
  5.8 0.0 copy-done.6
  5.8 0.0 copy-done.7
  5.8 0.0 copy-done.8
  5.9 0.0 copy-start.1
  5.9 0.0 copy-start.3
  5.9 15.3 %grid_chunk.1 = (f32[48,16,128]{2,1,0:T(8,128)S(1)}, f32[48,16,128]{2,1,0:T(8,128)S(1)}) custom-call(s32[1]{0:T(128)} %bitcast.section_ref.refs_0_, f32[96]{0:T(128)S(1)} %copy-done.5, f32[16,16,128]{2,1,0:T(8,128)S(1)} %gains.1.refs_2_, f32[48,2,2,16,128]{4,3,2,1,0:T(8,128)S(1)} %get-tuple-element.14.refs_3_, ...), custom_call_target="tpu_custom_call" | custom-call | flops 14400000000 | bytes 4800000 | tf_op jit(solution)/shard_map/grid_chunk/pallas_call | solution.py:450
  21.2 0.2 collective-permute-start.1
  21.4 0.0 copy-done.1
  21.4 3.3 %index.1 = (s32[96]{0:T(128)S(1)}, s32[128]{0:T(128)S(1)}) custom-call(s32[96]{0:T(128)S(1)} %copy-done.3, s32[16384]{0:T(1024)S(1)} %copy-done.1), custom_call_target="tpu_custom_call" | custom-call | flops 1000000 | bytes 1000000 | tf_op jit(solution)/shard_map/index/pallas_call | solution.py:442
  24.6 1.1 %pack.1.refs_0_ = f32[2112,128]{1,0:T(8,128)S(1)} custom-call(s32[1]{0:T(128)} %bitcast.section_ref.refs_0_, s32[96]{0:T(128)S(1)} %get-tuple-element.9.row_ref, s32[128]{0:T(128)S(1)} %get-tuple-element.10.slot_ref, f32[48,16,128]{2,1,0:T(8,128)S(1)} %get-tuple-element.11.refs_0_), custom_call_target="tpu_custom_call" | custom-call | flops 100000000 | bytes 1000000 | tf_op jit(solution)/shard_map/pack/pallas_call | solution.py:471
  25.7 0.0 collective-permute-done.1.refs_1_
  25.7 0.8 %pack_more.1 = f32[2112,128]{1,0:T(8,128)S(1)} custom-call(s32[1]{0:T(128)} %bitcast.section_ref.refs_0_, s32[96]{0:T(128)S(1)} %get-tuple-element.9.row_ref, f32[2112,128]{1,0:T(8,128)S(1)} %pack.1.refs_0_, f32[48,16,128]{2,1,0:T(8,128)S(1)} %collective-permute-done.1.refs_1_), custom_call_target="tpu_custom_call" | custom-call | flops 1000000 | bytes 1000000 | tf_op jit(solution)/shard_map/pack_more/pallas_call | solution.py:474
  26.6 30.9 %all_to_all.5 = f32[64,1,4224]{2,1,0:T(1,128)S(1)} all-to-all(f32[64,1,4224]{2,1,0:T(1,128)S(1)} %bitcast.10), channel_id=1, replica_groups=mesh['section'=2,'grid'=64] {'grid'}, dimensions={0} | all-to-all | bytes 2162688 | tf_op jit(solution)/shard_map/all_to_all | solution.py:477
  57.5 1.9 %unpack.1 = f32[256,2048]{1,0:T(8,128)} custom-call(f32[2112,128]{1,0:T(8,128)S(1)} %bitcast.9), custom_call_target="tpu_custom_call" | custom-call | flops 1000000 | bytes 1000000 | tf_op jit(solution)/shard_map/unpack/pallas_call | solution.py:480
  (6 shorter events, 0.0 us)
Async XLA Ops:
  0.0 2.4 %copy-start = (f32[512,128]{1,0:T(8,128)S(1)}, f32[512,128]{1,0:T(8,128)}, u32[]{:S(2)}) copy-start(f32[512,128]{1,0:T(8,128)} %jones_ref.1) | copy-start | bytes 786436
  0.0 2.4 %copy-start.2 = (s32[2,96]{1,0:T(2,128)S(1)}, s32[2,96]{1,0:T(2,128)}, u32[]{:S(2)}) copy-start(s32[2,96]{1,0:T(2,128)} %stations_ref.1) | copy-start | bytes 2308
  0.0 5.8 %copy-start.4 = (f32[96,2,128]{2,1,0:T(2,128)S(1)}, f32[96,2,128]{2,1,0:T(2,128)}, u32[]{:S(2)}) copy-start(f32[96,2,128]{2,1,0:T(2,128)} %param.11) | copy-start | bytes 294916
  0.0 5.8 %copy-start.5 = (f32[96]{0:T(128)S(1)}, f32[96]{0:T(128)}, u32[]{:S(2)}) copy-start(f32[96]{0:T(128)} %refs_1_.1) | copy-start | bytes 1156
  0.0 5.8 %copy-start.6 = (bf16[768,256]{1,0:T(8,128)(2,1)S(1)}, bf16[768,256]{1,0:T(8,128)(2,1)}, u32[]{:S(2)}) copy-start(bf16[768,256]{1,0:T(8,128)(2,1)} %constant.23.clone.refs_7_) | copy-start | bytes 1179652
  0.0 5.8 %copy-start.7 = (f32[2,32,128]{2,1,0:T(8,128)S(1)}, f32[2,32,128]{2,1,0:T(8,128)}, u32[]{:S(2)}) copy-start(f32[2,32,128]{2,1,0:T(8,128)} %constant.22.clone.refs_6_) | copy-start | bytes 98308
  0.0 5.8 %copy-start.8 = (bf16[64,192]{1,0:T(8,128)(2,1)S(1)}, bf16[64,192]{1,0:T(8,128)(2,1)}, u32[]{:S(2)}) copy-start(bf16[64,192]{1,0:T(8,128)(2,1)} %constant.24.clone.refs_8_) | copy-start | bytes 73732
  2.3 3.5 %collective-permute-start = (f32[48,2,2,16,128]{4,3,2,1,0:T(8,128)S(1)}, f32[48,2,2,16,128]{4,3,2,1,0:T(8,128)S(1)}, u32[]{:S(2)}, u32[]{:S(2)}) collective-permute-start(f32[48,2,2,16,128]{4,3,2,1,0:T(8,128)S(1)} %get-tuple-element.13), channel_id=1, source_target_pairs={{0,64},{64,0},{1,65},{65,1},{2,66},{66,2},{3,67},{67,3},{4,68},{68... | collective-permute-start | bytes 4718600 | tf_op jit(solution)/shard_map/ppermute | solution.py:431
  5.9 15.5 %copy-start.1 = (s32[16384]{0:T(1024)S(1)}, s32[16384]{0:T(1024)}, u32[]{:S(2)}) copy-start(s32[16384]{0:T(1024)} %owner_ref.1) | copy-start | bytes 196612
  5.9 15.5 %copy-start.3 = (s32[96]{0:T(128)S(1)}, s32[96]{0:T(128)}, u32[]{:S(2)}) copy-start(s32[96]{0:T(128)} %tile_ref.1) | copy-start | bytes 1156
  21.2 4.6 %collective-permute-start.1 = (f32[48,16,128]{2,1,0:T(8,128)S(1)}, f32[48,16,128]{2,1,0:T(8,128)S(1)}, u32[]{:S(2)}, u32[]{:S(2)}) collective-permute-start(f32[48,16,128]{2,1,0:T(8,128)S(1)} %get-tuple-element.12), channel_id=1, source_target_pairs={{0,64},{64,0},{1,65},{65,1},{2,66},{66,2},{3,67},{67,3},{4,68},{68... | collective-permute-start | bytes 1179656 | tf_op jit(solution)/shard_map/ppermute | solution.py:467

commit v3 on v2

--- a/solution.py
+++ b/solution.py
@@ -111,9 +111,16 @@
     ]
 
 
-def gains_kernel(section_ref, stations_ref, jones_ref, coef_ref, p_rows, q_rows, turned):
+def prep_kernel(section_ref, stations_ref, tile_ref, owner_any, jones_ref, vis_any, coef_ref, own_ref, row_ref, slot_ref,
+                p_rows, q_rows, turned, owner_ref, sems):
     section = section_ref[0]
-    half = stations_ref.shape[1] // 2
+    sub_count = tile_ref.shape[0]
+    half = sub_count // 2
+    owner_copy = pltpu.make_async_copy(owner_any, owner_ref, sems.at[0])
+    owner_copy.start()
+    own_copy = pltpu.make_async_copy(vis_any.at[0, pl.ds(section * half, half)], own_ref, sems.at[1])
+    own_copy.start()
+
     p_rows[...] = jnp.zeros_like(p_rows)
     q_rows[...] = jnp.zeros_like(q_rows)
 
@@ -147,9 +154,6 @@
         for place in range(8):
             coef_ref[kind * 8 + place] = turned[pl.ds(place, 16, stride=8), :]
 
-
-def index_kernel(tile_ref, owner_ref, row_ref, slot_ref):
-    sub_count = tile_ref.shape[0]
     tiles_dev = owner_ref.shape[0] // (slot_ref.shape[0] // 2)
     shift = tiles_dev.bit_length() - 1
     assert tiles_dev == 1 << shift
@@ -160,24 +164,25 @@
         return carry
 
     lax.fori_loop(0, slot_ref.shape[0] // 4, clear, 0)
+    owner_copy.wait()
 
     def place_item(step, carry):
-        for k in range(8):
-            item = step * 8 + k
-            position = owner_ref[tile_ref[item]]
+        positions = [owner_ref[tile_ref[step * 8 + k]] for k in range(8)]
+        for k, position in enumerate(positions):
             target = 2 * (position >> shift)
             slot = position & (tiles_dev - 1)
             first = slot_ref[target]
             row = target + jnp.where((first == -1) | (first == slot), 0, 1)
             slot_ref[row] = slot
-            row_ref[item] = row
+            row_ref[step * 8 + k] = row
         return carry
 
     lax.fori_loop(0, sub_count // 8, place_item, 0)
+    own_copy.wait()
 
 
 def grid_kernel(chunk_start, section_ref, w_ref, coef_ref, own_ref, peer_ref, uv_ref, pixel_ref, right_ref, left_ref,
-                mine_ref, other_ref, bcast, rolled, wave_rows, totals):
+                mine_ref, other_ref, bcast, rolled, wave_rows, totals, finished):
     section = section_ref[0]
     groups = mine_ref.shape[0] // GROUP
     half = w_ref.shape[0] // 2
@@ -201,8 +206,9 @@
                 for kind in range(2):
                     column = (row ^ section) ^ kind
                     source = own_ref if row == 0 else peer_ref
-                    vis_real = source[first + g, column, 0]
-                    vis_imag = source[first + g, column, 1]
+                    at = first + g + (chunk_start if row == 0 else 0)
+                    vis_real = source[at, column, 0]
+                    vis_imag = source[at, column, 1]
                     for pol in range(2):
                         place = kind * 8 + (pol ^ section) * 4 + (row ^ section) * 2
                         cr = jnp.broadcast_to(rolled[place][:, g : g + 1], (16, 128))
@@ -225,6 +231,7 @@
                 real, imag = corr[pol]
                 bcast[g, pol * 16 : pol * 16 + 16] = real * turn_cos + imag * turn_sin
                 bcast[g, 32 + pol * 16 : 48 + pol * 16] = imag * turn_cos - real * turn_sin
+            yield
 
             waves = []
             for axis, cell in enumerate((u_row, v_row)):
@@ -243,6 +250,7 @@
                 cos_1 = cos_0 * cos_d - sin_0 * sin_d
                 sin_1 = sin_0 * cos_d + cos_0 * sin_d
                 waves.append([cos_0, sin_0, cos_1, sin_1, cos_d + cos_d])
+            yield
             total = None
             for pair in range(8):
                 left_parts, right_parts = [], []
@@ -268,71 +276,95 @@
                     preferred_element_type=jnp.float32,
                 )
                 total = part if total is None else total + part
-            totals[group & 1, g] = total
+                yield
+            totals[g] = total
 
     def imaging(group):
         first = group * GROUP
-        lane32 = lax.broadcasted_iota(jnp.int32, (32, 128), 1)
         lane16 = lax.broadcasted_iota(jnp.int32, (16, 128), 1)
-        sums = swap_groups(
-            [totals[group & 1, g] for g in range(GROUP)], lane32 < 64, (lane32 & 32) == 32
-        )
         upper = (lane16 & 16) == 16
         sign = jnp.where(upper, -1.0, 1.0)
+        low_half, odd_quarter = lane16 < 64, (lane16 & 32) == 32
         w_first = section * half + chunk_start + first
         w_row = jnp.where(
             lane < 64,
             jnp.where(lane < 32, w_ref[w_first], w_ref[w_first + 1]),
             jnp.where(lane < 96, w_ref[w_first + 2], w_ref[w_first + 3]),
         )
-        w_turns = pixel_ref[0].reshape(4, 8, 128) * w_row[None]
-        w_sin, w_cos = sincos_turns(w_turns.reshape(32, 128))
-        w_sin, w_cos = w_sin * pixel_ref[1], w_cos * pixel_ref[1]
+        w_row = jnp.concatenate([w_row, w_row], 0)
+        turned = []
+        for k in range(2):
+            rows = slice(k * 16, k * 16 + 16)
+            w_sin, w_cos = sincos_turns(pixel_ref[0, rows] * w_row)
+            turned.append((w_sin * pixel_ref[1, rows], w_cos * pixel_ref[1, rows]))
+            yield
+        parts = []
+        for k in range(2):
+            sums = swap_groups(
+                [finished[g, k * 16 : k * 16 + 16] for g in range(GROUP)], low_half, odd_quarter
+            )
+            yield
+            for value in sums:
+                parts.append(
+                    (
+                        jnp.where(upper, pltpu.roll(value, 16, 1), value),
+                        sign * jnp.where(upper, value, pltpu.roll(value, 112, 1)),
+                    )
+                )
+                yield
         fields = []
         for pol in range(2):
-            cos_part, sin_part = [], []
-            for value in (sums[pol][:16], sums[2 + pol][:16], sums[pol][16:], sums[2 + pol][16:]):
-                cos_part.append(jnp.where(upper, pltpu.roll(value, 16, 1), value))
-                sin_part.append(sign * jnp.where(upper, value, pltpu.roll(value, 112, 1)))
-            even_re = cos_part[0] - sin_part[1]
-            even_im = cos_part[1] + sin_part[0]
-            odd_re = cos_part[3] + sin_part[2]
-            odd_im = cos_part[2] - sin_part[3]
-            image_re = jnp.concatenate([even_re - odd_re, even_re + odd_re], 0)
-            image_im = jnp.concatenate([even_im + odd_im, even_im - odd_im], 0)
-            fields.append(
-                jnp.concatenate(
-                    [image_re * w_cos - image_im * w_sin, image_re * w_sin + image_im * w_cos], 1
+            xa, xb, ya, yb = parts[pol], parts[2 + pol], parts[4 + pol], parts[6 + pol]
+            even_re, even_im = xa[0] - xb[1], xb[0] + xa[1]
+            odd_re, odd_im = yb[0] + ya[1], ya[0] - yb[1]
+            for k in range(2):
+                w_sin, w_cos = turned[k]
+                image_re = even_re - odd_re if k == 0 else even_re + odd_re
+                image_im = even_im + odd_im if k == 0 else even_im - odd_im
+                fields.append(
+                    jnp.concatenate(
+                        [image_re * w_cos - image_im * w_sin, image_re * w_sin + image_im * w_cos], 1
+                    )
                 )
+                yield
+        pieces = []
+        for field in fields:
+            high, low = split_hi_lo(field)
+            pieces.append(jnp.concatenate([high, low, high], 1))
+            yield
+        rows = jnp.dot(jnp.concatenate(pieces, 0), right_ref[...], preferred_element_type=jnp.float32)
+        yield
+        for pol, out_ref in enumerate((mine_ref, other_ref)):
+            high, low = split_hi_lo(rows[pol * 32 : pol * 32 + 32])
+            stack = jnp.concatenate(
+                [high[:, :128], high[:, 128:], low[:, :128], low[:, 128:], high[:, :128], high[:, 128:]], 0
             )
-        high, low = split_hi_lo(jnp.concatenate(fields, 0))
-        rows = jnp.dot(
-            jnp.concatenate([high, low, high], 1), right_ref[...], preferred_element_type=jnp.float32
-        )
-        high, low = split_hi_lo(rows)
-        for pol, out_ref in enumerate((mine_ref, other_ref)):
-            top = slice(pol * 32, pol * 32 + 32)
-            stack = jnp.concatenate(
-                [high[top, :128], high[top, 128:], low[top, :128], low[top, 128:], high[top, :128], high[top, 128:]],
-                0,
-            )
+            yield
             uv = jnp.dot(left_ref[...], stack, preferred_element_type=jnp.float32)
+            yield
             for part in range(2):
-                parts = swap_groups(
+                outs = swap_groups(
                     [uv[part * 32 + k * 8 : part * 32 + k * 8 + 8] for k in range(4)], lane < 64, (lane & 32) == 32
                 )
                 for g in range(GROUP):
-                    out_ref[first + g, part * 8 : part * 8 + 8, :] = parts[g]
-
-    gridding(0)
+                    out_ref[first + g, part * 8 : part * 8 + 8, :] = outs[g]
+                yield
+
+    def run(work):
+        for _ in work:
+            pass
+
+    run(gridding(0))
 
     def both(group, carry):
-        imaging(group - 1)
-        gridding(group)
+        finished[...] = totals[...]
+        run(imaging(group - 1))
+        run(gridding(group))
         return carry
 
     lax.fori_loop(1, groups, both, 0)
-    imaging(groups - 1)
+    finished[...] = totals[...]
+    run(imaging(groups - 1))
 
 
 def pack_kernel(section_ref, row_ref, slot_ref, *refs):
@@ -398,6 +430,7 @@
 
 SMEM = pl.BlockSpec(memory_space=pltpu.SMEM)
 VMEM = pl.BlockSpec(memory_space=pltpu.VMEM)
+ANY = pl.BlockSpec(memory_space=pl.ANY)
 
 
 def call(kernel, name, out_shape, in_specs, out_specs, scratch=(), flops=1_000_000, moved=1_000_000, mib=8):
@@ -425,23 +458,25 @@
     shape_f32 = lambda *shape: jax.ShapeDtypeStruct(shape, jnp.float32)
     shape_i32 = lambda *shape: jax.ShapeDtypeStruct(shape, jnp.int32)
 
-    own, peers, start = [], [], 0
+    peers, start = [], 0
     for size in CHUNKS:
         rows = lax.dynamic_slice_in_dim(visibilities[0], (1 - section_index) * half + start, size, 0)
         peers.append(lax.ppermute(rows, "section", swap))
         start += size
-    start = 0
-    for size in CHUNKS:
-        own.append(lax.dynamic_slice_in_dim(visibilities[0], section_index * half + start, size, 0))
-        start += size
-
-    coefs = call(
-        gains_kernel, "gains", shape_f32(16, 16, 128), [SMEM, SMEM, VMEM], VMEM,
-        [pltpu.VMEM((128, 128), jnp.float32)] * 3,
-    )(section, stations, jones_gains)
-    row_index, slots = call(
-        index_kernel, "index", (shape_i32(sub_count), shape_i32(2 * grid_size)), [SMEM, SMEM], (SMEM, SMEM)
-    )(tile_ids, owner_map)
+    coefs, own, row_index, slots = call(
+        prep_kernel,
+        "prep",
+        (
+            shape_f32(16, 16, 128),
+            shape_f32(half, *visibilities.shape[2:]),
+            shape_i32(sub_count),
+            shape_i32(2 * grid_size),
+        ),
+        [SMEM, SMEM, SMEM, ANY, VMEM, ANY],
+        (VMEM, VMEM, SMEM, SMEM),
+        [pltpu.VMEM((128, 128), jnp.float32)] * 3
+        + [pltpu.SMEM(owner_map.shape, jnp.int32), pltpu.SemaphoreType.DMA((2,))],
+    )(section, stations, tile_ids, owner_map, jones_gains, visibilities)
 
     constants = [jnp.asarray(table) for table in tables(samples)]
     uv_rows = uv_coords.reshape(2 * sub_count, uv_coords.shape[2])
@@ -457,12 +492,13 @@
                 pltpu.VMEM((GROUP, 64, 128), jnp.float32),
                 pltpu.VMEM((16, 16, 128), jnp.float32),
                 pltpu.VMEM((56, 128), jnp.float32),
-                pltpu.VMEM((2, GROUP, 32, 128), jnp.float32),
+                pltpu.VMEM((GROUP, 32, 128), jnp.float32),
+                pltpu.VMEM((GROUP, 32, 128), jnp.float32),
             ],
             flops=size * 300_000_000,
             moved=size * 100_000,
             mib=12,
-        )(section, w_terms, coefs, own[chunk], peers[chunk], uv_rows, *constants)
+        )(section, w_terms, coefs, own, peers[chunk], uv_rows, *constants)
         mine.append(kept)
         theirs.append(lax.ppermute(other, "section", swap))
         start += size

time: 59.5 us -> 58.4 us (0.982)
  local copies, waits for them, and re-layouts: 2.33 us -> 4.07 us
  waiting for transfers between devices: 2.24 us -> 0.6 us
  Pallas kernels: 23.5 us -> 22.5 us
    unnamed x18 -> x20, local copies, waits for them, and re-layouts: 0.04 us -> 2.32 us
    ppermute x1, waiting for transfers between devices: 2.24 us -> 0.01 us  [shards(): peers.append(lax.ppermute(rows, 'section', swap))]
    pallas_call x2 -> x1, Pallas kernels: 4.4 us -> 3.57 us  [shards(): call(prep_kernel, 'prep', (shape_f32(16, 16, 128), shape_f32(half, *visib...]
  transfers between devices with their start and end apart: 2 -> 2, of which waited for: 1 -> 1; matrix products, arithmetic and copies ran while one was open for 0% -> 0% of each run, Pallas kernels for 9% -> 8%
where the time goes in v3:
time: 58.4 us; the launch traced here: 58.2 us
  blocking collectives  30.7 us (53%)
  Pallas kernels  22.5 us (39%)
  local copies, waits for them, and re-layouts  4.07 us (7%)
  waiting for transfers between devices  0.6 us (1%)
    all_to_all x1, blocking collectives, shards(): lax.all_to_all(packed.reshape(grid_size, 1, 33 * 128), 'grid', split_axis...  30.7 us
    pallas_call x1, Pallas kernels, shards(): call(lambda *refs, start=start: grid_kernel(start, *refs), 'grid_chunk',...  15.2 us
    pallas_call x1, Pallas kernels, shards(): call(prep_kernel, 'prep', (shape_f32(16, 16, 128), shape_f32(half, *visib...  3.57 us
    unnamed x20, local copies, waits for them, and re-layouts  2.32 us
    pallas_call x1, Pallas kernels, shards(): call(unpack_kernel, 'unpack', shape_f32(tiles_dev, 2048), [VMEM], VMEM)  1.86 us
    dynamic_slice x1, local copies, waits for them, and re-layouts, shards(): lax.dynamic_slice_in_dim(visibilities[0], (1 - section_index) * half + st...  1.76 us
  transfers between devices with their start and end apart: 2, of which 1 were waited for; matrix products, arithmetic and copies ran while one was open for 0% of the time, Pallas kernels for 8%

profile of v3, /device:TPU:0, one launch (start us, length us, event | category | flops | bytes accessed | tf_op | source)
XLA Modules:
  0.0 58.2 jit_solution(10339190518639194215)
XLA Ops:
  0.0 0.0 copy-start
  0.0 0.0 copy-start.4
  0.0 1.8 %dynamic-slice_bitcast_fusion = f32[48,2,2,16,128]{4,3,2,1,0:T(8,128)S(1)} fusion(f32[1,96,2,2,16,128]{5,4,3,2,1,0:T(8,128)} %vis_any.1, s32[]{:T(128)S(6)} %select_n.3), kind=kLoop, calls=%fused_computation | loop fusion | bytes 3145732 | tf_op jit(solution)/shard_map/dynamic_slice | solution.py:463
  1.8 0.1 collective-permute-start
  1.9 0.5 copy-done
  2.4 0.0 copy-done.3
  2.4 0.0 copy-done.4
  2.4 0.9 %copy-done.1 = f32[512,128]{1,0:T(8,128)S(1)} copy-done((f32[512,128]{1,0:T(8,128)S(1)}, f32[512,128]{1,0:T(8,128)}, u32[]{:S(2)}) %copy-start.1) | copy-done | bytes 262168
  3.3 0.8 %copy-done.2 = s32[16384]{0:T(1024)S(1)} copy-done((s32[16384]{0:T(1024)S(1)}, s32[16384]{0:T(1024)}, u32[]{:S(2)}) %copy-start.2) | copy-done | bytes 65560
  4.2 0.0 copy-start.9
  4.2 3.6 %prep.1 = (f32[16,16,128]{2,1,0:T(8,128)S(1)}, f32[48,2,2,16,128]{4,3,2,1,0:T(8,128)S(1)}, s32[96]{0:T(128)S(1)}, s32[128]{0:T(128)S(1)}) custom-call(s32[1]{0:T(128)} %bitcast.section_ref.refs_0_, s32[2,96]{1,0:T(2,128)S(1)} %copy-done.3, s32[96]{0:T(128)S(1)} %copy-done.4, s32[16384]{0:T(1024)S(1)} %copy-done.2, f32[512,128]{1,0:T(8,128)S(1)} %copy-done.1, ...), custom_call_target="tpu_custom_call" | custom-call | flops 1000000 | bytes 1000000 | tf_op jit(solution)/shard_map/prep/pallas_call | solution.py:466
  7.8 0.0 collective-permute-done.refs_4_
  7.8 0.0 copy-done.5
  7.8 0.0 copy-done.6
  7.8 0.0 copy-done.7
  7.8 0.0 copy-done.8
  7.8 0.0 copy-done.9
  7.8 15.2 %grid_chunk.1 = (f32[48,16,128]{2,1,0:T(8,128)S(1)}, f32[48,16,128]{2,1,0:T(8,128)S(1)}) custom-call(s32[1]{0:T(128)} %bitcast.section_ref.refs_0_, f32[96]{0:T(128)S(1)} %copy-done.6, f32[16,16,128]{2,1,0:T(8,128)S(1)} %get-tuple-element.13.refs_2_, f32[48,2,2,16,128]{4,3,2,1,0:T(8,128)S(1)} %get-tuple-element.14.refs_3_, ...), custom_call_target="tpu_custom_call" | custom-call | flops 14400000000 | bytes 4800000 | tf_op jit(solution)/shard_map/grid_chunk/pallas_call | solution.py:485
  23.0 0.1 collective-permute-start.1
  23.1 1.1 %pack.1.refs_0_ = f32[2112,128]{1,0:T(8,128)S(1)} custom-call(s32[1]{0:T(128)} %bitcast.section_ref.refs_0_, s32[96]{0:T(128)S(1)} %get-tuple-element.11.row_ref, s32[128]{0:T(128)S(1)} %get-tuple-element.12.slot_ref, f32[48,16,128]{2,1,0:T(8,128)S(1)} %get-tuple-element.15.refs_0_), custom_call_target="tpu_custom_call" | custom-call | flops 100000000 | bytes 1000000 | tf_op jit(solution)/shard_map/pack/pallas_call | solution.py:507
  24.2 0.6 %collective-permute-done.1.refs_1_ = f32[48,16,128]{2,1,0:T(8,128)S(1)} collective-permute-done((f32[48,16,128]{2,1,0:T(8,128)S(1)}, f32[48,16,128]{2,1,0:T(8,128)S(1)}, u32[]{:S(2)}, u32[]{:S(2)}) %collective-permute-start.1) | collective-permute-done | bytes 393248 | tf_op jit(solution)/shard_map/ppermute | solution.py:503
  24.8 0.8 %pack_more.1 = f32[2112,128]{1,0:T(8,128)S(1)} custom-call(s32[1]{0:T(128)} %bitcast.section_ref.refs_0_, s32[96]{0:T(128)S(1)} %get-tuple-element.11.row_ref, f32[2112,128]{1,0:T(8,128)S(1)} %pack.1.refs_0_, f32[48,16,128]{2,1,0:T(8,128)S(1)} %collective-permute-done.1.refs_1_), custom_call_target="tpu_custom_call" | custom-call | flops 1000000 | bytes 1000000 | tf_op jit(solution)/shard_map/pack_more/pallas_call | solution.py:510
  25.6 30.7 %all_to_all.5 = f32[64,1,4224]{2,1,0:T(1,128)S(1)} all-to-all(f32[64,1,4224]{2,1,0:T(1,128)S(1)} %bitcast.8), channel_id=1, replica_groups=mesh['section'=2,'grid'=64] {'grid'}, dimensions={0} | all-to-all | bytes 2162688 | tf_op jit(solution)/shard_map/all_to_all | solution.py:513
  56.3 1.9 %unpack.1 = f32[256,2048]{1,0:T(8,128)} custom-call(f32[2112,128]{1,0:T(8,128)S(1)} %bitcast.7), custom_call_target="tpu_custom_call" | custom-call | flops 1000000 | bytes 1000000 | tf_op jit(solution)/shard_map/unpack/pallas_call | solution.py:516
  (7 shorter events, 0.0 us)
Async XLA Ops:
  0.0 2.4 %copy-start = (f32[1,96,2,2,16,128]{5,4,3,2,1,0:T(8,128)S(1)}, f32[1,96,2,2,16,128]{5,4,3,2,1,0:T(8,128)}, u32[]{:S(2)}) copy-start(f32[1,96,2,2,16,128]{5,4,3,2,1,0:T(8,128)} %vis_any.1) | copy-start | bytes 9437188
  0.0 2.4 %copy-start.3 = (s32[2,96]{1,0:T(2,128)S(1)}, s32[2,96]{1,0:T(2,128)}, u32[]{:S(2)}) copy-start(s32[2,96]{1,0:T(2,128)} %stations_ref.1) | copy-start | bytes 2308
  0.0 2.4 %copy-start.4 = (s32[96]{0:T(128)S(1)}, s32[96]{0:T(128)}, u32[]{:S(2)}) copy-start(s32[96]{0:T(128)} %tile_ref.1) | copy-start | bytes 1156
  1.8 6.0 %collective-permute-start = (f32[48,2,2,16,128]{4,3,2,1,0:T(8,128)S(1)}, f32[48,2,2,16,128]{4,3,2,1,0:T(8,128)S(1)}, u32[]{:S(2)}, u32[]{:S(2)}) collective-permute-start(f32[48,2,2,16,128]{4,3,2,1,0:T(8,128)S(1)} %dynamic-slice_bitcast_fusion), channel_id=1, source_target_pairs={{0,64},{64,0},{1,65},{65,1},{2,66},{66,2},{3,67},{67,3},{4,68},{68... | collective-permute-start | bytes 4718600 | tf_op jit(solution)/shard_map/ppermute | solution.py:464
  2.4 1.0 %copy-start.1 = (f32[512,128]{1,0:T(8,128)S(1)}, f32[512,128]{1,0:T(8,128)}, u32[]{:S(2)}) copy-start(f32[512,128]{1,0:T(8,128)} %jones_ref.1) | copy-start | bytes 786436
  3.3 0.8 %copy-start.2 = (s32[16384]{0:T(1024)S(1)}, s32[16384]{0:T(1024)}, u32[]{:S(2)}) copy-start(s32[16384]{0:T(1024)} %owner_any.1) | copy-start | bytes 196612
  4.2 3.6 %copy-start.5 = (f32[96,2,128]{2,1,0:T(2,128)S(1)}, f32[96,2,128]{2,1,0:T(2,128)}, u32[]{:S(2)}) copy-start(f32[96,2,128]{2,1,0:T(2,128)} %param.11) | copy-start | bytes 294916
  4.2 3.6 %copy-start.6 = (f32[96]{0:T(128)S(1)}, f32[96]{0:T(128)}, u32[]{:S(2)}) copy-start(f32[96]{0:T(128)} %refs_1_.1) | copy-start | bytes 1156
  4.2 3.6 %copy-start.7 = (bf16[768,256]{1,0:T(8,128)(2,1)S(1)}, bf16[768,256]{1,0:T(8,128)(2,1)}, u32[]{:S(2)}) copy-start(bf16[768,256]{1,0:T(8,128)(2,1)} %constant.22.clone.refs_7_) | copy-start | bytes 1179652
  4.2 3.6 %copy-start.8 = (bf16[64,192]{1,0:T(8,128)(2,1)S(1)}, bf16[64,192]{1,0:T(8,128)(2,1)}, u32[]{:S(2)}) copy-start(bf16[64,192]{1,0:T(8,128)(2,1)} %constant.23.clone.refs_8_) | copy-start | bytes 73732
  4.2 3.6 %copy-start.9 = (f32[2,32,128]{2,1,0:T(8,128)S(1)}, f32[2,32,128]{2,1,0:T(8,128)}, u32[]{:S(2)}) copy-start(f32[2,32,128]{2,1,0:T(8,128)} %constant.21.clone.refs_6_) | copy-start | bytes 98308
  23.0 1.8 %collective-permute-start.1 = (f32[48,16,128]{2,1,0:T(8,128)S(1)}, f32[48,16,128]{2,1,0:T(8,128)S(1)}, u32[]{:S(2)}, u32[]{:S(2)}) collective-permute-start(f32[48,16,128]{2,1,0:T(8,128)S(1)} %get-tuple-element.16), channel_id=1, source_target_pairs={{0,64},{64,0},{1,65},{65,1},{2,66},{66,2},{3,67},{67,3},{4,68},{68... | collective-permute-start | bytes 1179656 | tf_op jit(solution)/shard_map/ppermute | solution.py:503

commit v4 on v3

--- a/solution.py
+++ b/solution.py
@@ -111,15 +111,13 @@
     ]
 
 
-def prep_kernel(section_ref, stations_ref, tile_ref, owner_any, jones_ref, vis_any, coef_ref, own_ref, row_ref, slot_ref,
-                p_rows, q_rows, turned, owner_ref, sems):
+def prep_kernel(section_ref, stations_ref, jones_ref, *refs):
+    count = (len(refs) - 4) // 2
+    for source, target in zip(refs[:count], refs[count + 1 : 2 * count + 1]):
+        target[...] = source[...]
+    coef_ref, (p_rows, q_rows, turned) = refs[count], refs[2 * count + 1 :]
     section = section_ref[0]
-    sub_count = tile_ref.shape[0]
-    half = sub_count // 2
-    owner_copy = pltpu.make_async_copy(owner_any, owner_ref, sems.at[0])
-    owner_copy.start()
-    own_copy = pltpu.make_async_copy(vis_any.at[0, pl.ds(section * half, half)], own_ref, sems.at[1])
-    own_copy.start()
+    half = stations_ref.shape[1] // 2
 
     p_rows[...] = jnp.zeros_like(p_rows)
     q_rows[...] = jnp.zeros_like(q_rows)
@@ -154,43 +152,49 @@
         for place in range(8):
             coef_ref[kind * 8 + place] = turned[pl.ds(place, 16, stride=8), :]
 
-    tiles_dev = owner_ref.shape[0] // (slot_ref.shape[0] // 2)
+
+def clear_slots(slot_ref):
+    for target in range(slot_ref.shape[0]):
+        slot_ref[target] = -1
+
+
+def place_items(first, count, tile_ref, owner_ref, row_ref, slot_ref):
+    tiles_dev = owner_ref.shape[0] * 128 // (slot_ref.shape[0] // 2)
     shift = tiles_dev.bit_length() - 1
     assert tiles_dev == 1 << shift
-
-    def clear(step, carry):
-        for k in range(4):
-            slot_ref[step * 4 + k] = -1
-        return carry
-
-    lax.fori_loop(0, slot_ref.shape[0] // 4, clear, 0)
-    owner_copy.wait()
-
-    def place_item(step, carry):
-        positions = [owner_ref[tile_ref[step * 8 + k]] for k in range(8)]
-        for k, position in enumerate(positions):
-            target = 2 * (position >> shift)
-            slot = position & (tiles_dev - 1)
-            first = slot_ref[target]
-            row = target + jnp.where((first == -1) | (first == slot), 0, 1)
-            slot_ref[row] = slot
-            row_ref[step * 8 + k] = row
-        return carry
-
-    lax.fori_loop(0, sub_count // 8, place_item, 0)
-    own_copy.wait()
-
-
-def grid_kernel(chunk_start, section_ref, w_ref, coef_ref, own_ref, peer_ref, uv_ref, pixel_ref, right_ref, left_ref,
-                mine_ref, other_ref, bcast, rolled, wave_rows, totals, finished):
+    for k in range(count):
+        item = jnp.minimum(first + k, tile_ref.shape[0] - 1)
+        tile = tile_ref[item]
+        position = owner_ref[tile >> 7, tile & 127]
+        target = 2 * (position >> shift)
+        slot = position & (tiles_dev - 1)
+        known = slot_ref[target]
+        row = target + jnp.where((known == -1) | (known == slot), 0, 1)
+        slot_ref[row] = slot
+        row_ref[item] = row
+
+
+def grid_kernel(chunk_start, placing, section_ref, w_ref, coef_ref, own_ref, peer_ref, uv_ref, pixel_ref, right_ref,
+                left_ref, *refs):
+    if placing:
+        tile_ref, owner_any, mine_ref, other_ref, row_ref, slot_ref = refs[:6]
+        owner_ref, owner_sem = refs[-2:]
+        owner_copy = pltpu.make_async_copy(owner_any, owner_ref, owner_sem)
+        owner_copy.start()
+        clear_slots(slot_ref)
+    else:
+        mine_ref, other_ref = refs[:2]
+    start = 6 if placing else 2
+    bcast_all, rolled_all, rows_all, totals, finished = refs[start : start + 5]
     section = section_ref[0]
     groups = mine_ref.shape[0] // GROUP
     half = w_ref.shape[0] // 2
     lane = lax.broadcasted_iota(jnp.int32, (8, 128), 1)
     sub_lane = lax.broadcasted_iota(jnp.int32, (8, 128), 0).astype(jnp.float32)
 
-    def gridding(group):
+    def gridding(group, side):
         first = group * GROUP
+        bcast, rolled, wave_rows = bcast_all.at[side], rolled_all.at[side], rows_all.at[side]
         shift = lax.rem(128 - (chunk_start + first), 128)
         for place in range(16):
             rolled[place] = pltpu.roll(coef_ref[place], shift, 1)
@@ -206,7 +210,7 @@
                 for kind in range(2):
                     column = (row ^ section) ^ kind
                     source = own_ref if row == 0 else peer_ref
-                    at = first + g + (chunk_start if row == 0 else 0)
+                    at = first + g + (section * half + chunk_start if row == 0 else 0)
                     vis_real = source[at, column, 0]
                     vis_imag = source[at, column, 1]
                     for pol in range(2):
@@ -277,9 +281,9 @@
                 )
                 total = part if total is None else total + part
                 yield
-            totals[g] = total
-
-    def imaging(group):
+            totals[side, g] = total
+
+    def imaging(group, side):
         first = group * GROUP
         lane16 = lax.broadcasted_iota(jnp.int32, (16, 128), 1)
         upper = (lane16 & 16) == 16
@@ -301,7 +305,7 @@
         parts = []
         for k in range(2):
             sums = swap_groups(
-                [finished[g, k * 16 : k * 16 + 16] for g in range(GROUP)], low_half, odd_quarter
+                [finished[side, g, k * 16 : k * 16 + 16] for g in range(GROUP)], low_half, odd_quarter
             )
             yield
             for value in sums:
@@ -354,17 +358,32 @@
         for _ in work:
             pass
 
-    run(gridding(0))
-
-    def both(group, carry):
+    def image_pair(pair):
         finished[...] = totals[...]
-        run(imaging(group - 1))
-        run(gridding(group))
+        second = imaging(2 * pair + 1, 1)
+        for _ in imaging(2 * pair, 0):
+            next(second)
+        run(second)
+
+    def grid_pair(pair):
+        run(gridding(2 * pair, 0))
+        run(gridding(2 * pair + 1, 1))
+
+    pairs = groups // 2
+    grid_pair(0)
+    if placing:
+        owner_copy.wait()
+        each = -(-tile_ref.shape[0] // (pairs - 1))
+
+    def both(pair, carry):
+        if placing:
+            place_items((pair - 1) * each, each, tile_ref, owner_ref, row_ref, slot_ref)
+        image_pair(pair - 1)
+        grid_pair(pair)
         return carry
 
-    lax.fori_loop(1, groups, both, 0)
-    finished[...] = totals[...]
-    run(imaging(groups - 1))
+    lax.fori_loop(1, pairs, both, 0)
+    image_pair(pairs - 1)
 
 
 def pack_kernel(section_ref, row_ref, slot_ref, *refs):
@@ -383,29 +402,32 @@
         return carry
 
     lax.fori_loop(0, slot_ref.shape[0] // 4, note, 0)
-    add_rows(row_ref, section * half, width, refs[:-1], packed)
-
-
-def pack_more_kernel(section_ref, row_ref, *refs):
-    packed = refs[-1]
+    start = section * half
+    for values in refs[: len(CHUNKS)]:
+        add_rows(row_ref, start, width, values, packed)
+        start = start + values.shape[0]
+    start = (1 - section) * half
+    for values in refs[len(CHUNKS) : -1]:
+        add_rows(row_ref, start, width, values, packed)
+        start = start + values.shape[0]
+
+
+def pack_more_kernel(section_ref, row_ref, before_ref, values, packed):
     half = row_ref.shape[0] // 2
-    packed[...] = refs[0][...]
-    add_rows(row_ref, (1 - section_ref[0]) * half, 33, refs[1:-1], packed)
-
-
-def add_rows(row_ref, start, width, sources, packed):
-    for values in sources:
-
-        def add(step, carry, values=values, start=start):
-            for k in range(4):
-                item = step * 4 + k
-                row = row_ref[start + item]
-                top = (row >> 1) * width + (row & 1) * 16
-                packed[pl.ds(top, 16), :] = packed[pl.ds(top, 16), :] + values[item]
-            return carry
-
-        lax.fori_loop(0, values.shape[0] // 4, add, 0)
-        start = start + values.shape[0]
+    packed[...] = before_ref[...]
+    add_rows(row_ref, (2 - section_ref[0]) * half - values.shape[0], 33, values, packed)
+
+
+def add_rows(row_ref, start, width, values, packed):
+    def add(step, carry):
+        for k in range(4):
+            item = step * 4 + k
+            row = row_ref[start + item]
+            top = (row >> 1) * width + (row & 1) * 16
+            packed[pl.ds(top, 16), :] = packed[pl.ds(top, 16), :] + values[item]
+        return carry
+
+    lax.fori_loop(0, values.shape[0] // 4, add, 0)
 
 
 def unpack_kernel(received_ref, out_ref):
@@ -430,7 +452,7 @@
 
 SMEM = pl.BlockSpec(memory_space=pltpu.SMEM)
 VMEM = pl.BlockSpec(memory_space=pltpu.VMEM)
-ANY = pl.BlockSpec(memory_space=pl.ANY)
+HBM = pl.BlockSpec(memory_space=pltpu.HBM)
 
 
 def call(kernel, name, out_shape, in_specs, out_specs, scratch=(), flops=1_000_000, moved=1_000_000, mib=8):
@@ -460,56 +482,55 @@
 
     peers, start = [], 0
     for size in CHUNKS:
-        rows = lax.dynamic_slice_in_dim(visibilities[0], (1 - section_index) * half + start, size, 0)
-        peers.append(lax.ppermute(rows, "section", swap))
+        part = lax.dynamic_slice_in_dim(visibilities[0], (1 - section_index) * half + start, size, 0)
+        peers.append(lax.ppermute(part, "section", swap))
         start += size
-    coefs, own, row_index, slots = call(
+    passed = [jnp.asarray(table) for table in tables(samples)]
+    passed += [uv_coords.reshape(2 * sub_count, uv_coords.shape[2]), owner_map.reshape(-1, 128)]
+    coefs, *constants, uv_rows, owner_rows = call(
         prep_kernel,
         "prep",
-        (
-            shape_f32(16, 16, 128),
-            shape_f32(half, *visibilities.shape[2:]),
-            shape_i32(sub_count),
-            shape_i32(2 * grid_size),
-        ),
-        [SMEM, SMEM, SMEM, ANY, VMEM, ANY],
-        (VMEM, VMEM, SMEM, SMEM),
-        [pltpu.VMEM((128, 128), jnp.float32)] * 3
-        + [pltpu.SMEM(owner_map.shape, jnp.int32), pltpu.SemaphoreType.DMA((2,))],
-    )(section, stations, tile_ids, owner_map, jones_gains, visibilities)
-
-    constants = [jnp.asarray(table) for table in tables(samples)]
-    uv_rows = uv_coords.reshape(2 * sub_count, uv_coords.shape[2])
+        (shape_f32(16, 16, 128),) + tuple(jax.ShapeDtypeStruct(x.shape, x.dtype) for x in passed),
+        [SMEM, SMEM, VMEM] + [VMEM] * len(passed),
+        (VMEM,) * (1 + len(passed)),
+        [pltpu.VMEM((128, 128), jnp.float32)] * 3,
+    )(section, stations, jones_gains, *passed)
     mine, theirs, start = [], [], 0
     for chunk, size in enumerate(CHUNKS):
-        kept, other = call(
-            lambda *refs, start=start: grid_kernel(start, *refs),
+        placing = chunk == len(CHUNKS) - 1
+        results = call(
+            lambda *refs, start=start, placing=placing: grid_kernel(start, placing, *refs),
             "grid_chunk",
-            (shape_f32(size, 16, 128),) * 2,
-            [SMEM, SMEM] + [VMEM] * 7,
-            (VMEM, VMEM),
+            (shape_f32(size, 16, 128),) * 2 + ((shape_i32(sub_count), shape_i32(2 * grid_size)) if placing else ()),
+            [SMEM, SMEM] + [VMEM] * 7 + ([SMEM, HBM] if placing else []),
+            (VMEM, VMEM) + ((SMEM, SMEM) if placing else ()),
             [
-                pltpu.VMEM((GROUP, 64, 128), jnp.float32),
-                pltpu.VMEM((16, 16, 128), jnp.float32),
-                pltpu.VMEM((56, 128), jnp.float32),
-                pltpu.VMEM((GROUP, 32, 128), jnp.float32),
-                pltpu.VMEM((GROUP, 32, 128), jnp.float32),
-            ],
+                pltpu.VMEM((2, GROUP, 64, 128), jnp.float32),
+                pltpu.VMEM((2, 16, 16, 128), jnp.float32),
+                pltpu.VMEM((2, 56, 128), jnp.float32),
+                pltpu.VMEM((2, GROUP, 32, 128), jnp.float32),
+                pltpu.VMEM((2, GROUP, 32, 128), jnp.float32),
+            ]
+            + ([pltpu.SMEM(owner_rows.shape, jnp.int32), pltpu.SemaphoreType.DMA] if placing else []),
             flops=size * 300_000_000,
             moved=size * 100_000,
             mib=12,
-        )(section, w_terms, coefs, own, peers[chunk], uv_rows, *constants)
-        mine.append(kept)
-        theirs.append(lax.ppermute(other, "section", swap))
+        )(
+            section, w_terms, coefs, visibilities[0], peers[chunk], uv_rows, *constants,
+            *((tile_ids, owner_rows) if placing else ()),
+        )
+        mine.append(results[0])
+        theirs.append(lax.ppermute(results[1], "section", swap))
         start += size
+    row_index, slots = results[2:]
 
     packed_shape = shape_f32(33 * grid_size, 128)
     packed = call(
-        pack_kernel, "pack", packed_shape, [SMEM] * 3 + [VMEM] * len(CHUNKS), VMEM, flops=100_000_000
-    )(section, row_index, slots, *mine)
-    packed = call(
-        pack_more_kernel, "pack_more", packed_shape, [SMEM] * 2 + [VMEM] * (1 + len(CHUNKS)), VMEM
-    )(section, row_index, packed, *theirs)
+        pack_kernel, "pack", packed_shape, [SMEM] * 3 + [VMEM] * (2 * len(CHUNKS) - 1), VMEM, flops=100_000_000
+    )(section, row_index, slots, *mine, *theirs[:-1])
+    packed = call(pack_more_kernel, "pack_more", packed_shape, [SMEM] * 2 + [VMEM] * 2, VMEM)(
+        section, row_index, packed, theirs[-1]
+    )
     received = lax.all_to_all(
         packed.reshape(grid_size, 1, 33 * 128), "grid", split_axis=0, concat_axis=0, tiled=True
     ).reshape(33 * grid_size, 128)

time: 58.4 us -> 57.8 us (0.990)
  Pallas kernels: 22.5 us -> 18.6 us
  local copies, waits for them, and re-layouts: 4.07 us -> 6.88 us
    pallas_call x4, Pallas kernels: 20.7 us -> 16.7 us  [the longest x1 13.6 us: shards(): call(lambda *refs, start=start, placing=placing: grid_kernel(start, placi...]
    unnamed x20, local copies, waits for them, and re-layouts: 2.32 us -> 5.2 us
  transfers between devices with their start and end apart: 2 -> 2, of which waited for: 1 -> 1; matrix products, arithmetic and copies ran while one was open for 0% -> 0% of each run, Pallas kernels for 8% -> 4%
where the time goes in v4:
time: 57.8 us; the launch traced here: 57.4 us
  blocking collectives  30.9 us (53%)
  Pallas kernels  18.6 us (32%)
  local copies, waits for them, and re-layouts  6.88 us (12%)
  starting transfers between devices  0.66 us (1%)
    all_to_all x1, blocking collectives, shards(): lax.all_to_all(packed.reshape(grid_size, 1, 33 * 128), 'grid', split_axis...  30.9 us
    pallas_call x1, Pallas kernels, shards(): call(lambda *refs, start=start, placing=placing: grid_kernel(start, placi...  13.6 us
    unnamed x20, local copies, waits for them, and re-layouts  5.2 us
    pallas_call x1, Pallas kernels, shards(): call(unpack_kernel, 'unpack', shape_f32(tiles_dev, 2048), [VMEM], VMEM)  1.87 us
    dynamic_slice x1, local copies, waits for them, and re-layouts, shards(): lax.dynamic_slice_in_dim(visibilities[0], (1 - section_index) * half + st...  1.68 us
    pallas_call x1, Pallas kernels, shards(): call(prep_kernel, 'prep', (shape_f32(16, 16, 128),) + tuple((jax.ShapeDty...  1.18 us
  transfers between devices with their start and end apart: 2, of which 1 were waited for; matrix products, arithmetic and copies ran while one was open for 0% of the time, Pallas kernels for 4%

profile of v4, /device:TPU:0, one launch (start us, length us, event | category | flops | bytes accessed | tf_op | source)
XLA Modules:
  0.0 57.4 jit_solution(7453015478994030947)
XLA Ops:
  0.0 0.0 copy-start.7
  0.0 0.0 copy-start.8
  0.0 1.7 %dynamic-slice_bitcast_fusion = f32[48,2,2,16,128]{4,3,2,1,0:T(8,128)S(1)} fusion(f32[1,96,2,2,16,128]{5,4,3,2,1,0:T(8,128)} %param.10, s32[]{:T(128)S(6)} %select_n.3), kind=kLoop, calls=%fused_computation | loop fusion | bytes 3145732 | tf_op jit(solution)/shard_map/dynamic_slice | solution.py:485
  1.7 0.1 collective-permute-start
  1.8 0.0 copy-done.7
  1.8 0.0 copy-start.1
  1.8 1.0 %copy-done.1 = bf16[768,256]{1,0:T(8,128)(2,1)S(1)} copy-done((bf16[768,256]{1,0:T(8,128)(2,1)S(1)}, bf16[768,256]{1,0:T(8,128)(2,1)}, u32[]{:S(2)}) %copy-start.1) | copy-done | bytes 393240
  2.8 0.9 %copy-done.2 = f32[512,128]{1,0:T(8,128)S(1)} copy-done((f32[512,128]{1,0:T(8,128)S(1)}, f32[512,128]{1,0:T(8,128)}, u32[]{:S(2)}) %copy-start.2) | copy-done | bytes 262168
  3.7 0.9 %copy-done.3 = f32[96,2,128]{2,1,0:T(2,128)S(1)} copy-done((f32[96,2,128]{2,1,0:T(2,128)S(1)}, f32[96,2,128]{2,1,0:T(2,128)}, u32[]{:S(2)}) %copy-start.3) | copy-done | bytes 98328
  4.6 0.8 %copy-done.4 = s32[16384]{0:T(1024)S(1)} copy-done((s32[16384]{0:T(1024)S(1)}, s32[16384]{0:T(1024)}, u32[]{:S(2)}) %copy-start.4) | copy-done | bytes 65560
  5.5 0.8 %copy-done.5 = f32[2,32,128]{2,1,0:T(8,128)S(1)} copy-done((f32[2,32,128]{2,1,0:T(8,128)S(1)}, f32[2,32,128]{2,1,0:T(8,128)}, u32[]{:S(2)}) %copy-start.5) | copy-done | bytes 32792
  6.2 0.8 %copy-done.6 = bf16[64,192]{1,0:T(8,128)(2,1)S(1)} copy-done((bf16[64,192]{1,0:T(8,128)(2,1)S(1)}, bf16[64,192]{1,0:T(8,128)(2,1)}, u32[]{:S(2)}) %copy-start.6) | copy-done | bytes 24600
  7.0 1.2 %prep.1 = (f32[16,16,128]{2,1,0:T(8,128)S(1)}, f32[2,32,128]{2,1,0:T(8,128)S(1)}, bf16[768,256]{1,0:T(8,128)(2,1)S(1)}, bf16[64,192]{1,0:T(8,128)(2,1)S(1)}, f32...) custom-call(s32[1]{0:T(128)} %bitcast.section_ref.refs_0_, s32[2,96]{1,0:T(2,128)S(1)} %copy-done.7, ...), custom_call_target="tpu_custom_call" | custom-call | flops 1000000 | bytes 1000000 | tf_op jit(solution)/shard_map/prep/pallas_call | solution.py:490
  8.2 0.0 collective-permute-done.refs_4_
  8.2 0.0 copy-done
  8.2 0.0 copy-done.8
  8.2 0.0 copy-done.9
  8.2 13.6 %grid_chunk.1 = (f32[48,16,128]{2,1,0:T(8,128)S(1)}, f32[48,16,128]{2,1,0:T(8,128)S(1)}, s32[96]{0:T(128)S(1)}, s32[128]{0:T(128)S(1)}) custom-call(s32[1]{0:T(128)} %bitcast.section_ref.refs_0_, f32[96]{0:T(128)S(1)} %copy-done.8, f32[16,16,128]{2,1,0:T(8,128)S(1)} %get-tuple-element.15.refs_2_, f32[96,2,2,16,128]{4,3,2,1,0:T(8,128)S(1)} %bitcast.11, ...), custom_call_target="tpu_custom_call" | custom-call | flops 14400000000 | bytes 4800000 | tf_op jit(solution)/shard_map/grid_chunk/pallas_call | solution.py:501
  21.9 0.6 collective-permute-start.1
  22.4 1.1 %pack.1.before_ref = f32[2112,128]{1,0:T(8,128)S(1)} custom-call(s32[1]{0:T(128)} %bitcast.section_ref.refs_0_, s32[96]{0:T(128)S(1)} %get-tuple-element.21.row_ref, s32[128]{0:T(128)S(1)} %get-tuple-element.22.slot_ref, f32[48,16,128]{2,1,0:T(8,128)S(1)} %get-tuple-element.23.refs_0_), custom_call_target="tpu_custom_call" | custom-call | flops 100000000 | bytes 1000000 | tf_op jit(solution)/shard_map/pack/pallas_call | solution.py:528
  23.5 0.2 collective-permute-done.1.values
  23.8 0.8 %pack_more.1 = f32[2112,128]{1,0:T(8,128)S(1)} custom-call(s32[1]{0:T(128)} %bitcast.section_ref.refs_0_, s32[96]{0:T(128)S(1)} %get-tuple-element.21.row_ref, f32[2112,128]{1,0:T(8,128)S(1)} %pack.1.before_ref, f32[48,16,128]{2,1,0:T(8,128)S(1)} %collective-permute-done.1.values), custom_call_target="tpu_custom_call" | custom-call | flops 1000000 | bytes 1000000 | tf_op jit(solution)/shard_map/pack_more/pallas_call | solution.py:531
  24.6 30.9 %all_to_all.5 = f32[64,1,4224]{2,1,0:T(1,128)S(1)} all-to-all(f32[64,1,4224]{2,1,0:T(1,128)S(1)} %bitcast.10), channel_id=1, replica_groups=mesh['section'=2,'grid'=64] {'grid'}, dimensions={0} | all-to-all | bytes 2162688 | tf_op jit(solution)/shard_map/all_to_all | solution.py:534
  55.5 1.9 %unpack.1 = f32[256,2048]{1,0:T(8,128)} custom-call(f32[2112,128]{1,0:T(8,128)S(1)} %bitcast.9), custom_call_target="tpu_custom_call" | custom-call | flops 1000000 | bytes 1000000 | tf_op jit(solution)/shard_map/unpack/pallas_call | solution.py:537
  (7 shorter events, 0.0 us)
Async XLA Ops:
  0.0 1.8 %copy-start.7 = (s32[2,96]{1,0:T(2,128)S(1)}, s32[2,96]{1,0:T(2,128)}, u32[]{:S(2)}) copy-start(s32[2,96]{1,0:T(2,128)} %stations_ref.1) | copy-start | bytes 2308
  0.0 8.2 %copy-start = (f32[1,96,2,2,16,128]{5,4,3,2,1,0:T(8,128)S(1)}, f32[1,96,2,2,16,128]{5,4,3,2,1,0:T(8,128)}, u32[]{:S(2)}) copy-start(f32[1,96,2,2,16,128]{5,4,3,2,1,0:T(8,128)} %param.10) | copy-start | bytes 9437188
  0.0 8.2 %copy-start.8 = (f32[96]{0:T(128)S(1)}, f32[96]{0:T(128)}, u32[]{:S(2)}) copy-start(f32[96]{0:T(128)} %refs_1_.2) | copy-start | bytes 1156
  0.0 8.2 %copy-start.9 = (s32[96]{0:T(128)S(1)}, s32[96]{0:T(128)}, u32[]{:S(2)}) copy-start(s32[96]{0:T(128)} %refs_9_.1) | copy-start | bytes 1156
  1.7 6.5 %collective-permute-start = (f32[48,2,2,16,128]{4,3,2,1,0:T(8,128)S(1)}, f32[48,2,2,16,128]{4,3,2,1,0:T(8,128)S(1)}, u32[]{:S(2)}, u32[]{:S(2)}) collective-permute-start(f32[48,2,2,16,128]{4,3,2,1,0:T(8,128)S(1)} %dynamic-slice_bitcast_fusion), channel_id=1, source_target_pairs={{0,64},{64,0},{1,65},{65,1},{2,66},{66,2},{3,67},{67,3},{4,68},{68... | collective-permute-start | bytes 4718600 | tf_op jit(solution)/shard_map/ppermute | solution.py:486
  1.8 1.0 %copy-start.1 = (bf16[768,256]{1,0:T(8,128)(2,1)S(1)}, bf16[768,256]{1,0:T(8,128)(2,1)}, u32[]{:S(2)}) copy-start(bf16[768,256]{1,0:T(8,128)(2,1)} %constant.22.clone.refs_1_) | copy-start | bytes 1179652
  2.8 0.9 %copy-start.2 = (f32[512,128]{1,0:T(8,128)S(1)}, f32[512,128]{1,0:T(8,128)}, u32[]{:S(2)}) copy-start(f32[512,128]{1,0:T(8,128)} %jones_ref.1) | copy-start | bytes 786436
  3.7 0.9 %copy-start.3 = (f32[96,2,128]{2,1,0:T(2,128)S(1)}, f32[96,2,128]{2,1,0:T(2,128)}, u32[]{:S(2)}) copy-start(f32[96,2,128]{2,1,0:T(2,128)} %param.11) | copy-start | bytes 294916
  4.6 0.8 %copy-start.4 = (s32[16384]{0:T(1024)S(1)}, s32[16384]{0:T(1024)}, u32[]{:S(2)}) copy-start(s32[16384]{0:T(1024)} %param.15) | copy-start | bytes 196612
  5.5 0.8 %copy-start.5 = (f32[2,32,128]{2,1,0:T(8,128)S(1)}, f32[2,32,128]{2,1,0:T(8,128)}, u32[]{:S(2)}) copy-start(f32[2,32,128]{2,1,0:T(8,128)} %constant.21.clone.refs_0_) | copy-start | bytes 98308
  6.2 0.8 %copy-start.6 = (bf16[64,192]{1,0:T(8,128)(2,1)S(1)}, bf16[64,192]{1,0:T(8,128)(2,1)}, u32[]{:S(2)}) copy-start(bf16[64,192]{1,0:T(8,128)(2,1)} %constant.23.clone.refs_2_) | copy-start | bytes 73732
  21.9 1.9 %collective-permute-start.1 = (f32[48,16,128]{2,1,0:T(8,128)S(1)}, f32[48,16,128]{2,1,0:T(8,128)S(1)}, u32[]{:S(2)}, u32[]{:S(2)}) collective-permute-start(f32[48,16,128]{2,1,0:T(8,128)S(1)} %get-tuple-element.24), channel_id=1, source_target_pairs={{0,64},{64,0},{1,65},{65,1},{2,66},{66,2},{3,67},{67,3},{4,68},{68... | collective-permute-start | bytes 1179656 | tf_op jit(solution)/shard_map/ppermute | solution.py:523
